TPU v7x, 32 devices: a whole 2x2x4 slice. The times are simulated.
32 devices in a mesh: dp: 4 (over z), context: 4 (over y, x), tensor: 2 (over core).
Axes of the slice: x: 2, y: 2, z: 4, core: 2. Of those that a mesh axis runs over, the one named last changes fastest.
Arguments:
- tokens: bfloat16 [4, 4096, 768], P('dp', 'context'), may hold values from -6 to 6
- prefix_length: int32 [4], P('dp'), may hold values from 409 to 2048
- cluster_order: int32 [4, 12, 4096], P('dp', 'tensor'), may hold values from 0 to 4095, as said below
- query_weight: bfloat16 [768, 768], P('dp', 'tensor'), may hold values from -0.3125 to 0.3125
- key_weight: bfloat16 [768, 768], P('dp', 'tensor'), may hold values from -0.3125 to 0.3125
- value_weight: bfloat16 [768, 768], P('dp', 'tensor'), may hold values from -0.21875 to 0.21875
- output_weight: bfloat16 [768, 768], P('tensor', 'dp'), may hold values from -0.625 to 0.625
- inner_weight: bfloat16 [768, 3072], P('dp', 'tensor'), may hold values from -0.21875 to 0.21875
- outer_weight: bfloat16 [3072, 768], P('tensor', 'dp'), may hold values from -0.109375 to 0.109375
- query_bias: float32 [768], P('tensor'), may hold values from -3 to 3
- value_bias: float32 [768], P('tensor'), may hold values from -3 to 3
- output_bias: float32 [768], replicated, may hold values from -2 to 2
- inner_bias: float32 [3072], P('tensor'), may hold values from -3 to 3
- outer_bias: float32 [768], replicated, may hold values from -2 to 2
- first_gain: float32 [768], replicated, may hold values from 0.5 to 1.5
- first_shift: float32 [768], replicated, may hold values from -2 to 2
- second_gain: float32 [768], replicated, may hold values from 0.5 to 1.5
- second_shift: float32 [768], replicated, may hold values from -2 to 2
- cotangent: bfloat16 [4, 4096, 768], P('dp', 'context'), may hold values from -6 to 6
Outputs:
- activations: bfloat16 [4, 4096, 768], P('dp', 'context')
- input_grad: bfloat16 [4, 4096, 768], P('dp', 'context')
- query_weight_grad: float32 [768, 768], P('dp', 'tensor')
- key_weight_grad: float32 [768, 768], P('dp', 'tensor')
- value_weight_grad: float32 [768, 768], P('dp', 'tensor')
- output_weight_grad: float32 [768, 768], P('tensor', 'dp')
- inner_weight_grad: float32 [768, 3072], P('dp', 'tensor')
- outer_weight_grad: float32 [3072, 768], P('tensor', 'dp')
- query_bias_grad: float32 [768], P('tensor')
- value_bias_grad: float32 [768], P('tensor')
- output_bias_grad: float32 [768], replicated
- inner_bias_grad: float32 [3072], P('tensor')
- outer_bias_grad: float32 [768], replicated
- first_gain_grad: float32 [768], replicated
- first_shift_grad: float32 [768], replicated
- second_gain_grad: float32 [768], replicated
- second_shift_grad: float32 [768], replicated
Inputs may be any that keep to these rules, and one draw needn't show every extreme that they name: `cluster_order`: the positions of a sequence form pieces of 1024: piece c is c * 1024 to (c + 1) * 1024 - 1. For each sequence and head the entries are a permutation of 0 to 4095, and the entry at slot k * 128 + c * 32 + r, with r < 32, lies in piece c.
All inputs are finite; a program needn't handle non-finite values.
Results may differ from a plain program's by a relative error of at most 0.02.
Values may be sent and summed in bfloat16 or wider, within the bound.
A program may use at most 128 MiB of HBM per device.

v0:
```python
import jax
import jax.numpy as jnp
from jax import lax
from jax.sharding import PartitionSpec as P

D = 768
HEAD_DIM = 64
CLUSTER = 128


norm_epsilon = 1e-12
masked_score = -1e30


def normalize(values):
    center = values - jnp.mean(values, axis=-1, keepdims=True)
    inverse_root = lax.rsqrt(jnp.mean(center * center, axis=-1, keepdims=True) + norm_epsilon)
    return (center * inverse_root, inverse_root)


def norm_backward(upstream, normed, inverse_root, gain):
    scaled = upstream * gain
    centered = scaled - jnp.mean(scaled, axis=-1, keepdims=True)
    return inverse_root * (centered - normed * jnp.mean(scaled * normed, axis=-1, keepdims=True))


def gelu_slope(inner_pre):
    normal_cdf = 0.5 * (1.0 + lax.erf(inner_pre * 0.7071067811865476))
    return normal_cdf + inner_pre * jnp.exp(-0.5 * inner_pre * inner_pre) * 0.3989422804014327


def token_sum(values):
    return jnp.sum(values.astype(jnp.float32), axis=(0, 1))


def send_rows(ordering, own_index, context_size):
    sequences, head_count, length = ordering.shape
    slab_rows = length // context_size
    share_rows = CLUSTER // context_size
    local_groups = slab_rows // CLUSTER
    shaped = ordering.reshape(
        sequences, head_count, context_size, local_groups, context_size, share_rows
    )
    own_rows = lax.dynamic_index_in_dim(shaped, own_index, axis=4, keepdims=False)
    own_rows = jnp.transpose(own_rows, (0, 1, 3, 2, 4)).reshape(sequences, head_count, slab_rows)
    return own_rows - own_index * slab_rows


def permute_rows(values, rows_sent, backward):
    sequences, head_count, slab_rows, width = values.shape
    flat_values = values.reshape(sequences * head_count, slab_rows, width)
    flat_rows = rows_sent.reshape(sequences * head_count, slab_rows)
    positions = lax.broadcasted_iota(jnp.int32, (1, slab_rows), 1)

    def one_head(pair):
        head_values, head_rows = pair
        table = (head_rows[:, None] == positions).astype(jnp.bfloat16)
        if backward:
            product = jnp.einsum(
                "rp,rw->pw", table, head_values, preferred_element_type=jnp.float32
            )
        else:
            product = jnp.dot(table, head_values, preferred_element_type=jnp.float32)
        return product.astype(jnp.bfloat16)

    moved = lax.map(one_head, (flat_values, flat_rows))
    return moved.reshape(sequences, head_count, slab_rows, width)


def pack_clusters(picked, context_size):
    sequences, head_count, slab_rows, head_width = picked.shape
    return picked.reshape(
        sequences,
        head_count,
        slab_rows // CLUSTER,
        context_size,
        CLUSTER // context_size * head_width,
    )


def send_layout(grouped, context_size):
    sequences, head_count, local_groups, cluster_rows, head_width = grouped.shape
    return grouped.reshape(
        sequences, head_count, local_groups, context_size, cluster_rows // context_size * head_width
    )


def cluster_view(received):
    sequences, head_count, local_groups, context_size, packed = received.shape
    return received.reshape(sequences, head_count, local_groups, CLUSTER, HEAD_DIM)


def flat_rows_view(received):
    sequences, head_count, local_groups, context_size, packed = received.shape
    return received.reshape(sequences, head_count, local_groups * CLUSTER, HEAD_DIM)


def masked_scores(grouped_query, grouped_key, places, prefix):
    score_scale = HEAD_DIM ** (-0.5)
    raw_scores = jnp.einsum(
        "shcqd,shckd->shcqk", grouped_query, grouped_key, preferred_element_type=jnp.float32
    )
    allowed = jnp.logical_or(
        places[..., None, :] <= places[..., :, None],
        places[..., None, :] < prefix[:, None, None, None, None],
    )
    return jnp.where(allowed, raw_scores * score_scale, masked_score)


def shards(
    tokens,
    prefix_length,
    cluster_order,
    query_weight,
    key_weight,
    value_weight,
    output_weight,
    inner_weight,
    outer_weight,
    query_bias,
    value_bias,
    output_bias,
    inner_bias,
    outer_bias,
    first_gain,
    first_shift,
    second_gain,
    second_shift,
    cotangent,
):
    context_size = lax.axis_size("context")
    own_index = lax.axis_index("context")
    sequences, slab_rows, model_width = tokens.shape
    full_query, full_key, full_value, full_output, full_inner, full_outer = (
        lax.all_gather(query_weight, "dp", axis=0, tiled=True),
        lax.all_gather(key_weight, "dp", axis=0, tiled=True),
        lax.all_gather(value_weight, "dp", axis=0, tiled=True),
        lax.all_gather(output_weight, "dp", axis=1, tiled=True),
        lax.all_gather(inner_weight, "dp", axis=0, tiled=True),
        lax.all_gather(outer_weight, "dp", axis=1, tiled=True),
    )
    head_count = full_query.shape[1] // HEAD_DIM
    query_heads = full_query.reshape(D, head_count, HEAD_DIM)
    key_heads = full_key.reshape(D, head_count, HEAD_DIM)
    value_heads = full_value.reshape(D, head_count, HEAD_DIM)
    output_heads = full_output.reshape(head_count, HEAD_DIM, D)

    def project(heads_weight):
        return jnp.einsum("std,dhe->shte", tokens, heads_weight, preferred_element_type=jnp.float32)

    query_rows = (project(query_heads) + query_bias.reshape(1, head_count, 1, HEAD_DIM)).astype(
        jnp.bfloat16
    )
    key_rows = project(key_heads).astype(jnp.bfloat16)
    value_rows = (project(value_heads) + value_bias.reshape(1, head_count, 1, HEAD_DIM)).astype(
        jnp.bfloat16
    )
    rows_sent = send_rows(cluster_order, own_index, context_size)
    places = lax.dynamic_slice_in_dim(cluster_order, own_index * slab_rows, slab_rows, axis=2)
    places = places.reshape(sequences, head_count, slab_rows // CLUSTER, CLUSTER)
    picked = permute_rows(
        jnp.concatenate((query_rows, key_rows, value_rows), axis=3), rows_sent, False
    )
    got_query, got_key, got_value = (
        lax.all_to_all(
            pack_clusters(picked[..., :HEAD_DIM], context_size),
            "context",
            split_axis=3,
            concat_axis=3,
            tiled=True,
        ),
        lax.all_to_all(
            pack_clusters(picked[..., HEAD_DIM : 2 * HEAD_DIM], context_size),
            "context",
            split_axis=3,
            concat_axis=3,
            tiled=True,
        ),
        lax.all_to_all(
            pack_clusters(picked[..., 2 * HEAD_DIM :], context_size),
            "context",
            split_axis=3,
            concat_axis=3,
            tiled=True,
        ),
    )
    got_query = cluster_view(got_query)
    got_key = cluster_view(got_key)
    got_value = cluster_view(got_value)
    scores = masked_scores(got_query, got_key, places, prefix_length)
    row_max = jnp.max(scores, axis=-1, keepdims=True)
    exponent = jnp.exp(scores - row_max)
    row_total = jnp.sum(exponent, axis=-1, keepdims=True)
    log_total = row_max + jnp.log(row_total)
    weights = (exponent / row_total).astype(jnp.bfloat16)
    mixed_cluster = jnp.einsum(
        "shcqk,shckd->shcqd", weights, got_value, preferred_element_type=jnp.float32
    ).astype(jnp.bfloat16)
    returned = lax.all_to_all(
        send_layout(mixed_cluster, context_size), "context", split_axis=3, concat_axis=3, tiled=True
    )
    mixed_heads = permute_rows(flat_rows_view(returned), rows_sent, True)
    attention_part = jnp.einsum(
        "shte,hed->std", mixed_heads, output_heads, preferred_element_type=jnp.float32
    )
    branch = (
        lax.psum(attention_part.astype(jnp.bfloat16), "tensor").astype(jnp.float32) + output_bias
    )
    first_normed, first_root = normalize(tokens.astype(jnp.float32) + branch)
    first_norm = first_normed * first_gain + first_shift
    first_low = first_norm.astype(jnp.bfloat16)
    inner_pre = (
        jnp.einsum("std,df->stf", first_low, full_inner, preferred_element_type=jnp.float32)
        + inner_bias
    )
    activated = jax.nn.gelu(inner_pre, approximate=False).astype(jnp.bfloat16)
    feed_part = jnp.einsum("stf,fd->std", activated, full_outer, preferred_element_type=jnp.float32)
    feed_out = lax.psum(feed_part.astype(jnp.bfloat16), "tensor").astype(jnp.float32) + outer_bias
    second_normed, second_root = normalize(first_norm + feed_out)
    activations = (second_normed * second_gain + second_shift).astype(jnp.bfloat16)
    upstream = cotangent.astype(jnp.float32)
    second_gain_grad = token_sum(upstream * second_normed)
    second_shift_grad = token_sum(upstream)
    second_in_grad = norm_backward(upstream, second_normed, second_root, second_gain)
    feed_grad = second_in_grad.astype(jnp.bfloat16)
    outer_bias_grad = token_sum(feed_grad)
    outer_weight_grad = jnp.einsum(
        "stf,std->fd", activated, feed_grad, preferred_element_type=jnp.float32
    )
    act_grad = jnp.einsum("std,fd->stf", feed_grad, full_outer, preferred_element_type=jnp.float32)
    inner_grad = (act_grad * gelu_slope(inner_pre)).astype(jnp.bfloat16)
    inner_bias_grad = token_sum(inner_grad)
    inner_weight_grad = jnp.einsum(
        "std,stf->df", first_low, inner_grad, preferred_element_type=jnp.float32
    )
    first_part = jnp.einsum(
        "stf,df->std", inner_grad, full_inner, preferred_element_type=jnp.float32
    )
    first_grad = second_in_grad + lax.psum(first_part.astype(jnp.bfloat16), "tensor").astype(
        jnp.float32
    )
    first_gain_grad = token_sum(first_grad * first_normed)
    first_shift_grad = token_sum(first_grad)
    summed_grad = norm_backward(first_grad, first_normed, first_root, first_gain)
    branch_grad = summed_grad.astype(jnp.bfloat16)
    output_bias_grad = token_sum(branch_grad)
    output_weight_grad = jnp.einsum(
        "shte,std->hed", mixed_heads, branch_grad, preferred_element_type=jnp.float32
    ).reshape(head_count * HEAD_DIM, D)
    mixed_grad = jnp.einsum(
        "std,hed->shte", branch_grad, output_heads, preferred_element_type=jnp.float32
    ).astype(jnp.bfloat16)
    got_grad = cluster_view(
        lax.all_to_all(
            pack_clusters(permute_rows(mixed_grad, rows_sent, False), context_size),
            "context",
            split_axis=3,
            concat_axis=3,
            tiled=True,
        )
    )
    scores = masked_scores(got_query, got_key, places, prefix_length)
    probs = jnp.exp(scores - log_total)
    prob_grad = jnp.einsum(
        "shcqd,shckd->shcqk", got_grad, got_value, preferred_element_type=jnp.float32
    )
    value_grad = jnp.einsum(
        "shcqk,shcqd->shckd",
        probs.astype(jnp.bfloat16),
        got_grad,
        preferred_element_type=jnp.float32,
    ).astype(jnp.bfloat16)
    score_grad = (
        probs
        * (prob_grad - jnp.sum(probs * prob_grad, axis=-1, keepdims=True))
        * HEAD_DIM ** (-0.5)
    ).astype(jnp.bfloat16)
    query_grad = jnp.einsum(
        "shcqk,shckd->shcqd", score_grad, got_key, preferred_element_type=jnp.float32
    ).astype(jnp.bfloat16)
    key_grad = jnp.einsum(
        "shcqk,shcqd->shckd", score_grad, got_query, preferred_element_type=jnp.float32
    ).astype(jnp.bfloat16)
    back_query, back_key, back_value = (
        lax.all_to_all(
            send_layout(query_grad, context_size),
            "context",
            split_axis=3,
            concat_axis=3,
            tiled=True,
        ),
        lax.all_to_all(
            send_layout(key_grad, context_size), "context", split_axis=3, concat_axis=3, tiled=True
        ),
        lax.all_to_all(
            send_layout(value_grad, context_size),
            "context",
            split_axis=3,
            concat_axis=3,
            tiled=True,
        ),
    )
    restored = permute_rows(
        jnp.concatenate(
            (flat_rows_view(back_query), flat_rows_view(back_key), flat_rows_view(back_value)),
            axis=3,
        ),
        rows_sent,
        True,
    )
    back_query = restored[..., :HEAD_DIM]
    back_key = restored[..., HEAD_DIM : 2 * HEAD_DIM]
    back_value = restored[..., 2 * HEAD_DIM :]
    query_bias_grad = jnp.sum(back_query.astype(jnp.float32), axis=(0, 2)).reshape(
        head_count * HEAD_DIM
    )
    value_bias_grad = jnp.sum(back_value.astype(jnp.float32), axis=(0, 2)).reshape(
        head_count * HEAD_DIM
    )
    query_weight_grad = jnp.einsum(
        "std,shte->dhe", tokens, back_query, preferred_element_type=jnp.float32
    ).reshape(D, head_count * HEAD_DIM)
    key_weight_grad = jnp.einsum(
        "std,shte->dhe", tokens, back_key, preferred_element_type=jnp.float32
    ).reshape(D, head_count * HEAD_DIM)
    value_weight_grad = jnp.einsum(
        "std,shte->dhe", tokens, back_value, preferred_element_type=jnp.float32
    ).reshape(D, head_count * HEAD_DIM)
    input_part = jnp.einsum(
        "shte,dhe->std", back_query, query_heads, preferred_element_type=jnp.float32
    )
    input_part = input_part + jnp.einsum(
        "shte,dhe->std", back_key, key_heads, preferred_element_type=jnp.float32
    )
    input_part = input_part + jnp.einsum(
        "shte,dhe->std", back_value, value_heads, preferred_element_type=jnp.float32
    )
    input_grad = (
        summed_grad + lax.psum(input_part.astype(jnp.bfloat16), "tensor").astype(jnp.float32)
    ).astype(jnp.bfloat16)
    small_sums = lax.psum(
        (
            query_bias_grad,
            value_bias_grad,
            output_bias_grad,
            inner_bias_grad,
            outer_bias_grad,
            first_gain_grad,
            first_shift_grad,
            second_gain_grad,
            second_shift_grad,
        ),
        ("dp", "context"),
    )
    owned = (
        lax.psum_scatter(
            query_weight_grad.astype(jnp.bfloat16), "dp", scatter_dimension=0, tiled=True
        ).astype(jnp.float32),
        lax.psum_scatter(
            key_weight_grad.astype(jnp.bfloat16), "dp", scatter_dimension=0, tiled=True
        ).astype(jnp.float32),
        lax.psum_scatter(
            value_weight_grad.astype(jnp.bfloat16), "dp", scatter_dimension=0, tiled=True
        ).astype(jnp.float32),
        lax.psum_scatter(
            output_weight_grad.astype(jnp.bfloat16), "dp", scatter_dimension=1, tiled=True
        ).astype(jnp.float32),
        lax.psum_scatter(
            inner_weight_grad.astype(jnp.bfloat16), "dp", scatter_dimension=0, tiled=True
        ).astype(jnp.float32),
        lax.psum_scatter(
            outer_weight_grad.astype(jnp.bfloat16), "dp", scatter_dimension=1, tiled=True
        ).astype(jnp.float32),
    )
    owned = (
        lax.psum(owned[0].astype(jnp.bfloat16), "context").astype(jnp.float32),
        lax.psum(owned[1].astype(jnp.bfloat16), "context").astype(jnp.float32),
        lax.psum(owned[2].astype(jnp.bfloat16), "context").astype(jnp.float32),
        lax.psum(owned[3].astype(jnp.bfloat16), "context").astype(jnp.float32),
        lax.psum(owned[4].astype(jnp.bfloat16), "context").astype(jnp.float32),
        lax.psum(owned[5].astype(jnp.bfloat16), "context").astype(jnp.float32),
    )
    return (
        activations,
        input_grad,
        owned[0],
        owned[1],
        owned[2],
        owned[3],
        owned[4],
        owned[5],
        small_sums[0],
        small_sums[1],
        small_sums[2],
        small_sums[3],
        small_sums[4],
        small_sums[5],
        small_sums[6],
        small_sums[7],
        small_sums[8],
    )


def solution(mesh):
    placed = (
        P("dp", "context", None),
        P("dp"),
        P("dp", "tensor", None),
        P("dp", "tensor"),
        P("dp", "tensor"),
        P("dp", "tensor"),
        P("tensor", "dp"),
        P("dp", "tensor"),
        P("tensor", "dp"),
        P("tensor"),
        P("tensor"),
        P(),
        P("tensor"),
        P(),
        P(),
        P(),
        P(),
        P(),
        P("dp", "context", None),
    )
    return jax.shard_map(
        shards,
        mesh=mesh,
        in_specs=placed,
        out_specs=(
            P("dp", "context", None),
            P("dp", "context", None),
            P("dp", "tensor"),
            P("dp", "tensor"),
            P("dp", "tensor"),
            P("tensor", "dp"),
            P("dp", "tensor"),
            P("tensor", "dp"),
            P("tensor"),
            P("tensor"),
            P(),
            P("tensor"),
            P(),
            P(),
            P(),
            P(),
            P(),
        ),
        check_vma=False,
    )
```

profile of v0, /device:TPU:0, one launch (start us, length us, event | category | flops | bytes accessed | tf_op | source)
XLA Modules:
  0.0 821.3 jit_solution(16589285212470608762)
XLA Ops:
  9.8 18.6 %all_gather.18 = bf16[768,384]{1,0:T(8,128)(2,1)S(1)} all-gather(bf16[192,384]{1,0:T(8,128)(2,1)} %param.30), channel_id=1, replica_groups=mesh['dp'=4,'context'=4,'tensor'=2] {'dp'}, dimensions={0}, use_global_device_ids=true | all-gather | bytes 737280 | tf_op jit(solution)/shard_map/all_gather | solution.py:135
  28.7 16.7 %all_gather.20 = bf16[768,384]{1,0:T(8,128)(2,1)S(1)} all-gather(bf16[192,384]{1,0:T(8,128)(2,1)S(1)} %copy-done.23), channel_id=1, replica_groups=mesh['dp'=4,'context'=4,'tensor'=2] {'dp'}, dimensions={0}, use_global_device_ids=true | all-gather | bytes 737280 | tf_op jit(solution)/shard_map/all_gather | solution.py:137
  45.8 15.6 %all_gather.19 = bf16[768,384]{1,0:T(8,128)(2,1)S(1)} all-gather(bf16[192,384]{1,0:T(8,128)(2,1)S(1)} %copy-done.24), channel_id=1, replica_groups=mesh['dp'=4,'context'=4,'tensor'=2] {'dp'}, dimensions={0}, use_global_device_ids=true | all-gather | bytes 737280 | tf_op jit(solution)/shard_map/all_gather | solution.py:136
  69.5 17.3 %while.44 = (s32[]{:T(128)}, bf16[6,1024,192]{1,2,0:T(8,128)(2,1)}, s32[6,1024]{1,0:T(8,128)S(1)}, bf16[6,1024,192]{1,2,0:T(8,128)(2,1)}, s32[]{:T(128)}) while((s32[]{:T(128)}, bf16[6,1024,192]{1,2,0:T(8,128)(2,1)}, s32[6,1024]{1,0:T(8,128)S(1)}, bf16[6,1024,192]{1,2,0:T(8,128)(2,1)}, s32[]{:T(128)}) %tuple.101), condition=%wide.region_1.2_spmd.clone, body=%wide.region_0.1_spmd.clone.sunk | while | flops 403898368 | bytes 799809 | solution.py:66
  162.6 15.0 %all_gather.21 = bf16[384,768]{0,1:T(8,128)(2,1)S(1)} all-gather(bf16[384,192]{0,1:T(8,128)(2,1)S(1)} %copy-done.25), channel_id=1, replica_groups=mesh['dp'=4,'context'=4,'tensor'=2] {'dp'}, dimensions={1}, use_global_device_ids=true | all-gather | bytes 737280 | tf_op jit(solution)/shard_map/all_gather | solution.py:138
  181.5 11.6 %while.45 = (s32[]{:T(128)}, bf16[6,1024,64]{1,2,0:T(8,128)(2,1)S(1)}, s32[6,1024]{1,0:T(8,128)S(1)}, bf16[6,1024,64]{2,1,0:T(8,128)(2,1)}, s32[]{:T(128)}) while((s32[]{:T(128)}, bf16[6,1024,64]{1,2,0:T(8,128)(2,1)S(1)}, s32[6,1024]{1,0:T(8,128)S(1)}, bf16[6,1024,64]{2,1,0:T(8,128)(2,1)}, s32[]{:T(128)}) %tuple.140), condition=%wide.region_5.6_spmd.clone, body=%wide.region_4.5_spmd.clone.sunk | while | flops 135331840 | bytes 406593 | solution.py:66
  196.9 20.8 %all-reduce.8.cloned.1.call-done = bf16[1,1024,768]{2,1,0:T(8,128)(2,1)} async-done(((bf16[1,1024,768]{2,1,0:T(8,128)(2,1)}), bf16[1,1024,768]{2,1,0:T(8,128)(2,1)}) %all-reduce.8.cloned.1.call-update) | async-done | bytes 1572880 | tf_op jit(solution)/shard_map/psum | solution.py:207
  220.7 28.4 %all-gather.3.cloned.1.call-done = bf16[768,1536]{1,0:T(8,128)(2,1)} async-done(((bf16[192,1536]{1,0:T(8,128)(2,1)}), bf16[768,1536]{1,0:T(8,128)(2,1)}) %all-gather.3.cloned.1.call-update) | async-done | bytes 2359312 | tf_op jit(solution)/shard_map/all_gather | solution.py:139
  249.1 19.4 %fusion.43 = (bf16[1024,1536]{1,0:T(8,128)(2,1)}, f32[1024,1536]{1,0:T(8,128)}) fusion(f32[1536]{0:T(1024)S(1)} %copy-done.36, bf16[768,1536]{1,0:T(8,128)(2,1)} %all-gather.3.cloned.1.call-done, f32[768]{0:T(1024)S(1)} %copy-done.31, f32[768]{0:T(1024)S(1)} %copy-done.27, f32[1024]{0:T(1024)S(1)} %add_rsqrt_fusion.1, ...), kind=kOutput, calls=%fused_computation.49 | convolution fusion | flops 2526806016 | bytes 14965760 | tf_op jit(solution)/shard_map/std,df->stf/dot_general | solution.py:213
  268.5 30.7 %all-gather.5.cloned.1.call-done = bf16[1536,768]{0,1:T(8,128)(2,1)} async-done(((bf16[1536,192]{0,1:T(8,128)(2,1)}), bf16[1536,768]{0,1:T(8,128)(2,1)}) %all-gather.5.cloned.1.call-update) | async-done | bytes 2359312 | tf_op jit(solution)/shard_map/all_gather | solution.py:140
  306.1 18.8 %all-reduce.10.cloned.1.call-done = bf16[1,1024,768]{2,1,0:T(8,128)(2,1)} async-done(((bf16[1,1024,768]{2,1,0:T(8,128)(2,1)}), bf16[1,1024,768]{2,1,0:T(8,128)(2,1)}) %all-reduce.10.cloned.1.call-update) | async-done | bytes 1572880 | tf_op jit(solution)/shard_map/psum | solution.py:218
  343.3 21.7 %all-reduce.12.cloned.1.call-done = bf16[1,1024,768]{2,1,0:T(8,128)(2,1)} async-done(((bf16[1,1024,768]{2,1,0:T(8,128)(2,1)}), bf16[1,1024,768]{2,1,0:T(8,128)(2,1)}) %all-reduce.12.cloned.1.call-update) | async-done | bytes 1572880 | tf_op jit(solution)/shard_map/psum | solution.py:239
  375.0 15.5 %while.46 = (s32[]{:T(128)}, bf16[6,1024,64]{1,2,0:T(8,128)(2,1)}, s32[6,1024]{1,0:T(8,128)S(1)}, bf16[6,1024,64]{1,2,0:T(8,128)(2,1)}, s32[]{:T(128)}) while((s32[]{:T(128)}, bf16[6,1024,64]{1,2,0:T(8,128)(2,1)}, s32[6,1024]{1,0:T(8,128)S(1)}, bf16[6,1024,64]{1,2,0:T(8,128)(2,1)}, s32[]{:T(128)}) %tuple.141), condition=%wide.region_18.19_spmd.clone, body=%wide.region_17.18_spmd.clone.sunk | while | flops 135331840 | bytes 275521 | solution.py:66
  403.5 11.6 %all-to-all-done.4 = bf16[1,6,8,4,2048]{4,2,1,0,3:T(8,128)(2,1)} async-done(((bf16[1,6,8,4,2048]{4,2,1,0,3:T(8,128)(2,1)}), bf16[1,6,8,4,2048]{4,2,1,0,3:T(8,128)(2,1)}, u32[]{:S(2)}, u32[]{:S(2)}) %all-to-all-start.4) | async-done | bytes 786464 | tf_op jit(solution)/shard_map/all_to_all | solution.py:254
  426.0 7.5 fusion.124
  446.3 7.7 fusion.127
  510.0 17.2 %while.47 = (s32[]{:T(128)}, bf16[6,1024,192]{1,2,0:T(8,128)(2,1)}, s32[6,1024]{1,0:T(8,128)S(1)}, bf16[6,1024,192]{2,1,0:T(8,128)(2,1)}, s32[]{:T(128)}) while((s32[]{:T(128)}, bf16[6,1024,192]{1,2,0:T(8,128)(2,1)}, s32[6,1024]{1,0:T(8,128)S(1)}, bf16[6,1024,192]{2,1,0:T(8,128)(2,1)}, s32[]{:T(128)}) %tuple.142), condition=%wide.region_21.22_spmd.clone, body=%wide.region_20.21_spmd.clone.sunk | while | flops 403898368 | bytes 930881 | solution.py:66
  548.3 7.4 convolution_convert_fusion.1
  570.5 10.9 %reduce-scatter.21.cloned.1.call-done = bf16[192,384]{1,0:T(8,128)(2,1)} async-done(((bf16[768,384]{1,0:T(8,128)(2,1)}), bf16[192,384]{1,0:T(8,128)(2,1)}) %reduce-scatter.21.cloned.1.call-update) | async-done | bytes 147472
  583.1 21.7 %reduce-scatter.23.cloned.1.call-done = bf16[192,384]{1,0:T(8,128)(2,1)} async-done(((bf16[768,384]{1,0:T(8,128)(2,1)}), bf16[192,384]{1,0:T(8,128)(2,1)}) %reduce-scatter.23.cloned.1.call-update) | async-done | bytes 147472
  606.5 21.1 %reduce-scatter.13.cloned.1.call-done = bf16[384,192]{0,1:T(8,128)(2,1)} async-done(((bf16[384,768]{0,1:T(8,128)(2,1)}), bf16[384,192]{0,1:T(8,128)(2,1)}) %reduce-scatter.13.cloned.1.call-update) | async-done | bytes 147472 | tf_op jit(solution)/shard_map/reduce_scatter | solution.py:365
  627.6 48.3 %reduce-scatter.15.cloned.1.call-done = bf16[192,1536]{1,0:T(8,128)(2,1)} async-done(((bf16[768,1536]{1,0:T(8,128)(2,1)}), bf16[192,1536]{1,0:T(8,128)(2,1)}) %reduce-scatter.15.cloned.1.call-update) | async-done | bytes 589840 | tf_op jit(solution)/shard_map/reduce_scatter | solution.py:368
  675.9 49.2 %reduce-scatter.17.cloned.1.call-done = bf16[1536,192]{0,1:T(8,128)(2,1)} async-done(((bf16[1536,768]{0,1:T(8,128)(2,1)}), bf16[1536,192]{0,1:T(8,128)(2,1)}) %reduce-scatter.17.cloned.1.call-update) | async-done | bytes 589840 | tf_op jit(solution)/shard_map/reduce_scatter | solution.py:371
  726.9 76.2 %all-reduce = (f32[384]{0:T(512)}, f32[384]{0:T(512)}, f32[768]{0:T(1024)}, f32[1536]{0:T(1024)}, f32[768]{0:T(1024)}, /*index=5*/f32[768]{0:T(1024)}, f32[768]{0:T(1024)}, f32[768]{0:T(1024)}, f32[768]{0:T(1024)}) all-reduce(f32[384]{0:T(512)S(1)} %reshape.528, ...), channel_id=1, replica_groups=mesh['dp'=4,'context'=4,'tensor'=2] {'dp','context'}, use_global_device_ids=true, to_apply=%region_36.37 | all-reduce | flops 6912 | bytes 55296 | tf_op jit(solution)/shard_map/psum | solution.py:341
  (287 shorter events, 336.7 us)
Async XLA Ops:
  9.5 53.0 %copy-start = (bf16[1,1024,768]{2,1,0:T(8,128)(2,1)S(1)}, bf16[1,1024,768]{2,1,0:T(8,128)(2,1)}, u32[]{:S(2)}) copy-start(bf16[1,1024,768]{2,1,0:T(8,128)(2,1)} %param.27) | copy-start | bytes 4718596
  96.0 15.5 %all-to-all-start = ((bf16[1,6,8,4,2048]{4,2,1,0,3:T(8,128)(2,1)}), bf16[1,6,8,4,2048]{4,2,1,0,3:T(8,128)(2,1)}, u32[]{:S(2)}, u32[]{:S(2)}) async-start(bf16[1,6,8,4,2048]{4,2,1,0,3:T(8,128)(2,1)} %copy.86), calls=%async_computation | async-start | bytes 1572864 | tf_op jit(solution)/shard_map/all_to_all | solution.py:165
  111.5 15.9 %all-to-all-start.1 = ((bf16[1,6,8,4,2048]{4,2,1,0,3:T(8,128)(2,1)}), bf16[1,6,8,4,2048]{4,2,1,0,3:T(8,128)(2,1)}, u32[]{:S(2)}, u32[]{:S(2)}) async-start(bf16[1,6,8,4,2048]{4,2,1,0,3:T(8,128)(2,1)} %copy.89), calls=%async_computation.1 | async-start | bytes 1572864 | tf_op jit(solution)/shard_map/all_to_all | solution.py:172
  127.3 12.9 %all-to-all-start.2 = ((bf16[1,6,8,4,2048]{4,2,1,0,3:T(8,128)(2,1)}), bf16[1,6,8,4,2048]{4,2,1,0,3:T(8,128)(2,1)S(1)}, u32[]{:S(2)}, u32[]{:S(2)}) async-start(bf16[1,6,8,4,2048]{4,2,1,0,3:T(8,128)(2,1)} %copy.94), calls=%async_computation.2 | async-start | bytes 1572864 | tf_op jit(solution)/shard_map/all_to_all | solution.py:179
  158.5 20.2 %all-to-all-start.3 = ((bf16[1,6,8,4,2048]{4,2,1,0,3:T(8,128)(2,1)}), bf16[1,6,8,4,2048]{4,2,1,0,3:T(8,128)(2,1)S(1)}, u32[]{:S(2)}, u32[]{:S(2)}) async-start(bf16[1,6,8,4,2048]{4,2,1,0,3:T(8,128)(2,1)} %copy.99), calls=%async_computation.3 | async-start | bytes 1572864 | tf_op jit(solution)/shard_map/all_to_all | solution.py:199
  162.6 55.1 %all-reduce.8.cloned.1.call-start = ((), (), s32[]{:S(2)}) async-start(), calls=%async_computation.14 | async-start | bytes 3145728 | tf_op jit(solution)/shard_map/psum | solution.py:207
  195.4 53.7 %all-gather.3.cloned.1.call-start = ((), (), s32[]{:S(2)}) async-start(), calls=%async_computation.15 | async-start | bytes 2949120 | tf_op jit(solution)/shard_map/all_gather | solution.py:139
  196.0 103.2 %all-gather.5.cloned.1.call-start = ((), (), s32[]{:S(2)}) async-start(), calls=%async_computation.16 | async-start | bytes 2949120 | tf_op jit(solution)/shard_map/all_gather | solution.py:140
  196.6 52.5 %copy-start.27 = (f32[768]{0:T(1024)S(1)}, f32[768]{0:T(1024)}, u32[]{:S(2)}) copy-start(f32[768]{0:T(1024)} %param.41) | copy-start | bytes 9220
  196.6 52.5 %copy-start.31 = (f32[768]{0:T(1024)S(1)}, f32[768]{0:T(1024)}, u32[]{:S(2)}) copy-start(f32[768]{0:T(1024)} %param.42) | copy-start | bytes 9220
  196.6 128.3 %all-reduce.10.cloned.1.call-start = ((), (), s32[]{:S(2)}) async-start(), calls=%async_computation.17 | async-start | bytes 3145728 | tf_op jit(solution)/shard_map/psum | solution.py:218
  305.6 59.5 %all-reduce.12.cloned.1.call-start = ((), (), s32[]{:S(2)}) async-start(), calls=%async_computation.18 | async-start | bytes 3145728 | tf_op jit(solution)/shard_map/psum | solution.py:239
  399.1 16.0 %all-to-all-start.4 = ((bf16[1,6,8,4,2048]{4,2,1,0,3:T(8,128)(2,1)}), bf16[1,6,8,4,2048]{4,2,1,0,3:T(8,128)(2,1)}, u32[]{:S(2)}, u32[]{:S(2)}) async-start(bf16[1,6,8,4,2048]{4,2,1,0,3:T(8,128)(2,1)} %copy.104), calls=%async_computation.4 | async-start | bytes 1572864 | tf_op jit(solution)/shard_map/all_to_all | solution.py:254
  442.1 20.5 %all-to-all-start.5 = ((bf16[1,6,8,4,2048]{4,2,1,0,3:T(8,128)(2,1)}), bf16[1,6,8,4,2048]{4,2,1,0,3:T(8,128)(2,1)}, u32[]{:S(2)}, u32[]{:S(2)}) async-start(bf16[1,6,8,4,2048]{4,2,1,0,3:T(8,128)(2,1)} %copy.111), calls=%async_computation.5 | async-start | bytes 1572864 | tf_op jit(solution)/shard_map/all_to_all | solution.py:285
  462.6 17.2 %all-to-all-start.6 = ((bf16[1,6,8,4,2048]{4,2,1,0,3:T(8,128)(2,1)}), bf16[1,6,8,4,2048]{4,2,1,0,3:T(8,128)(2,1)}, u32[]{:S(2)}, u32[]{:S(2)}) async-start(bf16[1,6,8,4,2048]{4,2,1,0,3:T(8,128)(2,1)} %copy.116), calls=%async_computation.6 | async-start | bytes 1572864 | tf_op jit(solution)/shard_map/all_to_all | solution.py:292
  479.8 16.8 %all-to-all-start.7 = ((bf16[1,6,8,4,2048]{4,2,1,0,3:T(8,128)(2,1)}), bf16[1,6,8,4,2048]{4,2,1,0,3:T(8,128)(2,1)}, u32[]{:S(2)}, u32[]{:S(2)}) async-start(bf16[1,6,8,4,2048]{4,2,1,0,3:T(8,128)(2,1)} %copy.121), calls=%async_computation.7 | async-start | bytes 1572864 | tf_op jit(solution)/shard_map/all_to_all | solution.py:295
  484.1 84.7 %reduce-scatter.19.cloned.1.call-start = ((), (), s32[]{:S(2)}) async-start(), calls=%async_computation.23 | async-start | bytes 737280
  534.0 47.4 %reduce-scatter.21.cloned.1.call-start = ((), (), s32[]{:S(2)}) async-start(), calls=%async_computation.24 | async-start | bytes 737280
  539.5 65.3 %reduce-scatter.23.cloned.1.call-start = ((), (), s32[]{:S(2)}) async-start(), calls=%async_computation.25 | async-start | bytes 737280
  544.9 82.7 %reduce-scatter.13.cloned.1.call-start = ((), (), s32[]{:S(2)}) async-start(), calls=%async_computation.20 | async-start | bytes 737280 | tf_op jit(solution)/shard_map/reduce_scatter | solution.py:365
  548.0 127.9 %reduce-scatter.15.cloned.1.call-start = ((), (), s32[]{:S(2)}) async-start(), calls=%async_computation.21 | async-start | bytes 2949120 | tf_op jit(solution)/shard_map/reduce_scatter | solution.py:368
  555.7 169.4 %reduce-scatter.17.cloned.1.call-start = ((), (), s32[]{:S(2)}) async-start(), calls=%async_computation.22 | async-start | bytes 2949120 | tf_op jit(solution)/shard_map/reduce_scatter | solution.py:371
  562.8 240.4 %all-reduce.14.cloned.1.call-start = ((), (), s32[]{:S(2)}) async-start(), calls=%async_computation.19 | async-start | bytes 3145728 | tf_op jit(solution)/shard_map/psum | solution.py:339
  568.7 237.3 %all-reduce.16.cloned.1.call-start = ((), (), s32[]{:S(2)}) async-start(), calls=%async_computation.26 | async-start | bytes 3833856 | tf_op jit(solution)/shard_map/psum | solution.py:376
  (37 other events, 393.4 us)
Sparse Core Ops, SparseCore 0:
  195.5 22.1 all-reduce.7
  305.7 19.0 all-reduce.9
  343.5 21.5 all-reduce.11
  568.8 21.9 all-reduce.13
  725.2 67.3 all-reduce.15
Sparse Core Ops, SparseCore 1:
  197.5 51.6 all-gather.2
  250.5 48.6 all-gather.4
  534.1 23.8 reduce-scatter.18
  560.8 20.5 reduce-scatter.20
  584.3 20.5 reduce-scatter.22
  607.1 20.4 reduce-scatter.12
  629.8 46.0 reduce-scatter.14
  678.0 47.0 reduce-scatter.16
where the time goes:
time: 832 us; the launch traced here: 821 us
  waiting for transfers between devices  295 us (35%)
  matrix products  165 us (20%)
  blocking collectives  142 us (17%)
  local copies, waits for them, and re-layouts  131 us (16%)
  other arithmetic  36.3 us (4%)
  starting transfers between devices  34.8 us (4%)
  between operations  17.2 us (2%)
    psum x1, blocking collectives, shards(): lax.psum((query_bias_grad, value_bias_grad, output_bias_grad, inner_bias_...  76.2 us
    reduce_scatter x1, waiting for transfers between devices, shards(): lax.psum_scatter(outer_weight_grad.astype(jnp.bfloat16), 'dp', scatter_di...  49.2 us
    reduce_scatter x1, waiting for transfers between devices, shards(): lax.psum_scatter(inner_weight_grad.astype(jnp.bfloat16), 'dp', scatter_di...  48.3 us
    unnamed x16, waiting for transfers between devices  33.9 us
    dot_general x12, matrix products, one_head(): product = jnp.dot(table, head_values, preferred_element_type=jnp.float32)  32.7 us
    all_gather x1, waiting for transfers between devices, shards(): lax.all_gather(outer_weight, 'dp', axis=1, tiled=True)  30.7 us
    dot_general x12, matrix products, one_head(): jnp.einsum('rp,rw->pw', table, head_values, preferred_element_type=jnp.fl...  28.6 us
    all_gather x1, waiting for transfers between devices, shards(): lax.all_gather(inner_weight, 'dp', axis=0, tiled=True)  28.4 us
  transfers between devices with their start and end apart: 21, of which 13 were waited for; matrix products, arithmetic and copies ran while one was open for 16% of the time, Pallas kernels for 0%

commit v1 on v0

v1 whole, which is shorter than its diff:
```python
import functools

import jax
import jax.numpy as jnp
from jax import lax
from jax.experimental import pallas as pl
from jax.experimental.pallas import tpu as pltpu
from jax.sharding import PartitionSpec as P

HEAD_DIM = 64
CLUSTER = 128


norm_epsilon = 1e-12
masked_score = -1e30


def normalize(values):
    center = values - jnp.mean(values, axis=-1, keepdims=True)
    inverse_root = lax.rsqrt(jnp.mean(center * center, axis=-1, keepdims=True) + norm_epsilon)
    return (center * inverse_root, inverse_root)


def norm_backward(upstream, normed, inverse_root, gain):
    scaled = upstream * gain
    centered = scaled - jnp.mean(scaled, axis=-1, keepdims=True)
    return inverse_root * (centered - normed * jnp.mean(scaled * normed, axis=-1, keepdims=True))


def gelu_slope(inner_pre):
    normal_cdf = 0.5 * (1.0 + lax.erf(inner_pre * 0.7071067811865476))
    return normal_cdf + inner_pre * jnp.exp(-0.5 * inner_pre * inner_pre) * 0.3989422804014327


MESH = pl.DeviceIdType.MESH
BF16 = jnp.bfloat16
F32 = jnp.float32
PAIR = 2 * HEAD_DIM


def dot(a, b):
    return lax.dot_general(a, b, (((1,), (0,)), ((), ())), preferred_element_type=F32)


def dot_nt(a, b):
    return lax.dot_general(a, b, (((1,), (1,)), ((), ())), preferred_element_type=F32)


def dot_tn(a, b):
    return lax.dot_general(a, b, (((0,), (0,)), ((), ())), preferred_element_type=F32)


def remote(src, dst, send_sem, recv_sem, axis, index):
    return pltpu.make_async_remote_copy(
        src_ref=src,
        dst_ref=dst,
        send_sem=send_sem,
        recv_sem=recv_sem,
        device_id={axis: index},
        device_id_type=MESH,
    )


def meet(axes):
    barrier = pltpu.get_barrier_semaphore()
    count = 0
    for axis in axes:
        size, own = lax.axis_size(axis), lax.axis_index(axis)
        for step in range(1, size):
            pl.semaphore_signal(
                barrier,
                inc=1,
                device_id={axis: lax.rem(own + step, size)},
                device_id_type=MESH,
            )
            count += 1
    pl.semaphore_wait(barrier, count)


def low_lanes(shape):
    return lax.broadcasted_iota(jnp.int32, shape, 1) < HEAD_DIM


def one_hot(left, right):
    return jnp.where(left == right, 1.0, 0.0).astype(BF16)


def stack_pair(pair):
    low = low_lanes(pair.shape)
    zero = jnp.zeros_like(pair)
    return jnp.concatenate((jnp.where(low, pair, zero), jnp.where(low, zero, pair)), axis=0)


def fold_pair(stacked):
    rows = stacked.shape[0] // 2
    top, bottom = stacked[:rows], stacked[rows:]
    return jnp.where(low_lanes(top.shape), top, bottom)


def pair_scores(query2, key, mask2):
    raw = dot_nt(query2, key) * HEAD_DIM ** (-0.5)
    return jnp.where(mask2, raw, masked_score)


def pair_mask(cols_ref, rows_ref, pair, group, heads):
    row = pl.multiple_of(group * CLUSTER, CLUSTER)
    parts = []
    for head in (2 * pair, 2 * pair + 1):
        limit = cols_ref[pl.ds(row, CLUSTER), 8 + head : 9 + head]
        place = rows_ref[8 + head : 9 + head, pl.ds(row, CLUSTER)]
        parts.append(place <= limit)
    return parts


def forward_kernel(
    sizes,
    x_ref,
    query_ref,
    key_ref,
    value_ref,
    output_ref,
    inner_ref,
    outer_ref,
    cols_ref,
    rows_ref,
    query_bias_ref,
    value_bias_ref,
    output_bias_ref,
    first_in_ref,
    mixed_ref,
    got_ref,
    proj_ref,
    inner_full_ref,
    outer_full_ref,
    packed,
    sending,
    answer,
    returned,
    part,
    partner_part,
    own_sem,
    gather_send,
    forward_send,
    gather_recv,
    feed_send,
    feed_recv,
    move_send,
    move_recv,
    back_send,
    back_recv,
    pair_send,
    pair_recv,
):
    n_dp, n_ctx, pairs, gathers = sizes
    slab, width = x_ref.shape
    columns = pairs * PAIR
    dp, ctx, core = lax.axis_index("dp"), lax.axis_index("context"), lax.axis_index("tensor")
    chunk = slab // n_ctx
    groups = slab // CLUSTER
    share = CLUSTER // n_ctx
    shard = width // n_dp
    meet(("dp", "context", "tensor") if gathers else ("context", "tensor"))

    own_rows = pl.ds(pl.multiple_of(dp * shard, 16) if gathers else 0, shard)
    feed_copies = []
    if gathers:
        own = []
        for number, source in enumerate((query_ref, key_ref, value_ref, output_ref)):
            own.append(
                pltpu.make_async_copy(
                    source,
                    proj_ref.at[own_rows, pl.ds(number * columns, columns)],
                    own_sem.at[number],
                )
            )
        own.append(pltpu.make_async_copy(inner_ref, inner_full_ref.at[own_rows], own_sem.at[4]))
        own.append(pltpu.make_async_copy(outer_ref, outer_full_ref.at[own_rows], own_sem.at[5]))
        for copy in own:
            copy.start()

        def block(rows_of, block_number):
            rows = pl.ds(pl.multiple_of(rows_of * shard, 16), shard)
            lanes = pl.ds(pl.multiple_of(block_number * columns, columns), columns)
            return proj_ref.at[rows, lanes]

        for copy in own[:4]:
            copy.wait()
        gather_copies = []
        for step in range(1, n_dp):
            copy = remote(
                block(dp, ctx),
                block(dp, ctx),
                gather_send.at[step],
                gather_recv.at[ctx, dp],
                "dp",
                lax.rem(dp + step, n_dp),
            )
            copy.start()
            gather_copies.append(copy)
        for number, (source, full) in enumerate(
            ((inner_ref, inner_full_ref), (outer_ref, outer_full_ref))
        ):
            for step in range(1, n_dp):
                copy = remote(
                    source,
                    full.at[own_rows],
                    feed_send.at[number, step],
                    feed_recv.at[number, dp],
                    "dp",
                    lax.rem(dp + step, n_dp),
                )
                copy.start()
                feed_copies.append(copy)
        for step in range(1, n_dp):
            source = lax.rem(dp - step + n_dp, n_dp)
            remote(
                block(source, ctx),
                block(source, ctx),
                gather_send.at[step],
                gather_recv.at[ctx, source],
                "dp",
                source,
            ).wait_recv()
            for hop in range(1, n_ctx):
                copy = remote(
                    block(source, ctx),
                    block(source, ctx),
                    forward_send.at[step, hop],
                    gather_recv.at[ctx, source],
                    "context",
                    lax.rem(ctx + hop, n_ctx),
                )
                copy.start()
                gather_copies.append(copy)
        for hop in range(1, n_ctx):
            other = lax.rem(ctx - hop + n_ctx, n_ctx)
            for step in range(1, n_dp):
                source = lax.rem(dp - step + n_dp, n_dp)
                remote(
                    block(source, other),
                    block(source, other),
                    forward_send.at[step, hop],
                    gather_recv.at[other, source],
                    "context",
                    other,
                ).wait_recv()
    else:
        for number, source in enumerate((query_ref, key_ref, value_ref, output_ref)):
            proj_ref[:, number * columns : (number + 1) * columns] = source[...]

    def project(step, carry):
        rows = pl.ds(pl.multiple_of(step * chunk, chunk), chunk)
        values = dot(x_ref[rows, :], proj_ref[:, : 3 * columns])
        low = low_lanes((chunk, PAIR))
        for pair in range(pairs):
            lanes = slice(pair * PAIR, (pair + 1) * PAIR)
            query = values[:, lanes] + query_bias_ref[:, lanes]
            key = values[:, columns + pair * PAIR : columns + (pair + 1) * PAIR]
            value = (
                values[:, 2 * columns + pair * PAIR : 2 * columns + (pair + 1) * PAIR]
                + value_bias_ref[:, lanes]
            )
            first = jnp.where(low, query, pltpu.roll(key, HEAD_DIM, 1))
            second = jnp.where(low, pltpu.roll(query, HEAD_DIM, 1), key)
            packed[pair, rows, 0:PAIR] = first.astype(BF16)
            packed[pair, rows, PAIR : 2 * PAIR] = second.astype(BF16)
            packed[pair, rows, 2 * PAIR : 3 * PAIR] = value.astype(BF16)
        return carry

    lax.fori_loop(0, n_ctx, project, 0)

    own_share = pl.ds(pl.multiple_of(ctx * share, share), share)

    def pick(pair, target):
        rows = pl.ds(pl.multiple_of(target * chunk, chunk), chunk)
        positions = lax.broadcasted_iota(jnp.int32, (chunk, slab), 1)
        tables = [
            one_hot(cols_ref[rows, head : head + 1], positions) for head in (2 * pair, 2 * pair + 1)
        ]
        shared = packed[pair, :, 2 * PAIR : 3 * PAIR]
        even = dot(tables[0], jnp.concatenate((packed[pair, :, 0:PAIR], shared), axis=1))
        odd = dot(tables[1], jnp.concatenate((packed[pair, :, PAIR : 2 * PAIR], shared), axis=1))
        low = low_lanes((chunk, PAIR))
        query = jnp.where(low, even[:, :PAIR], pltpu.roll(odd[:, :PAIR], HEAD_DIM, 1))
        key = jnp.where(low, pltpu.roll(even[:, :PAIR], HEAD_DIM, 1), odd[:, :PAIR])
        value = jnp.where(low, even[:, PAIR:], odd[:, PAIR:])
        for number, piece in enumerate((query, key, value)):
            sending[pair, target, :, :, number * PAIR : (number + 1) * PAIR] = piece.astype(
                BF16
            ).reshape(groups, share, PAIR)

    def moved(pair, hop):
        target = lax.rem(ctx + hop, n_ctx)
        source = sending.at[pair, target]
        landing = got_ref.at[pair, :, own_share, :]
        if hop == 0:
            return pltpu.make_async_copy(source, landing, move_recv.at[pair, 0])
        return remote(
            source, landing, move_send.at[pair, hop], move_recv.at[pair, hop], "context", target
        )

    for pair in range(pairs):
        for hop in (*range(1, n_ctx), 0):
            pick(pair, lax.rem(ctx + hop, n_ctx))
            moved(pair, hop).start()

    def sent_back(pair, hop):
        target = lax.rem(ctx - hop + n_ctx, n_ctx)
        rows = pl.ds(pl.multiple_of(target * share, share), share)
        source = answer.at[pair, :, rows, :]
        landing = returned.at[pair, ctx]
        if hop == 0:
            return pltpu.make_async_copy(source, landing, back_recv.at[pair, 0])
        return remote(
            source, landing, back_send.at[pair, hop], back_recv.at[pair, hop], "context", target
        )

    for pair in range(pairs):
        for hop in range(n_ctx):
            copy = moved(pair, hop)
            if hop == 0:
                copy.wait()
            else:
                copy.wait_recv()

        def attend(group, carry):
            query2 = stack_pair(got_ref[pair, group, :, 0:PAIR])
            key = got_ref[pair, group, :, PAIR : 2 * PAIR]
            value = got_ref[pair, group, :, 2 * PAIR : 3 * PAIR]
            masks = pair_mask(cols_ref, rows_ref, pair, group, 2 * pairs)
            raw = dot_nt(query2, key) * HEAD_DIM ** (-0.5)
            scores = jnp.concatenate(
                [
                    jnp.where(mask, raw[i * CLUSTER : (i + 1) * CLUSTER], masked_score)
                    for i, mask in enumerate(masks)
                ],
                axis=0,
            )
            exponent = jnp.exp(scores - jnp.max(scores, axis=1, keepdims=True))
            total = jnp.sum(exponent, axis=1, keepdims=True)
            weights = (exponent / total).astype(BF16)
            answer[pair, group] = fold_pair(dot(weights, value)).astype(BF16)
            return carry

        lax.fori_loop(0, groups, attend, 0, unroll=2)
        for hop in (*range(1, n_ctx), 0):
            sent_back(pair, hop).start()

    for pair in range(pairs):
        for hop in range(n_ctx):
            copy = sent_back(pair, hop)
            if hop == 0:
                copy.wait()
            else:
                copy.wait_recv()

        def restore(step, carry):
            rows = pl.ds(pl.multiple_of(step * chunk, chunk), chunk)
            positions = lax.broadcasted_iota(jnp.int32, (chunk, slab), 0) + step * chunk
            values = returned[pair].reshape(slab, PAIR)
            even = dot(one_hot(rows_ref[2 * pair : 2 * pair + 1, :], positions), values)
            odd = dot(one_hot(rows_ref[2 * pair + 1 : 2 * pair + 2, :], positions), values)
            mixed_ref[rows, pair * PAIR : (pair + 1) * PAIR] = jnp.where(
                low_lanes(even.shape), even, odd
            ).astype(BF16)
            return carry

        lax.fori_loop(0, n_ctx, restore, 0)

    def exchange(step):
        rows = pl.ds(step * chunk, chunk)
        return remote(
            part.at[rows],
            partner_part.at[rows],
            pair_send.at[step],
            pair_recv.at[step],
            "tensor",
            1 - core,
        )

    for step in range(n_ctx):
        rows = slice(step * chunk, (step + 1) * chunk)
        part[rows, :] = dot_nt(mixed_ref[rows, :], proj_ref[:, 3 * columns :]).astype(BF16)
        exchange(step).start()
    for step in range(n_ctx):
        rows = slice(step * chunk, (step + 1) * chunk)
        exchange(step).wait_recv()
        branch = part[rows, :].astype(F32) + partner_part[rows, :].astype(F32)
        first_in_ref[rows, :] = x_ref[rows, :].astype(F32) + (branch + output_bias_ref[...])

    for step in range(n_ctx):
        exchange(step).wait_send()
    for pair in range(pairs):
        for hop in range(1, n_ctx):
            moved(pair, hop).wait_send()
            sent_back(pair, hop).wait_send()
    if gathers:
        for copy in gather_copies:
            copy.wait_send()
        for copy in feed_copies:
            copy.wait_send()
        for number, full in enumerate((inner_full_ref, outer_full_ref)):
            own[4 + number].wait()
            for step in range(1, n_dp):
                source = lax.rem(dp - step + n_dp, n_dp)
                rows = pl.ds(pl.multiple_of(source * shard, 16), shard)
                remote(
                    full.at[rows],
                    full.at[rows],
                    feed_send.at[number, step],
                    feed_recv.at[number, source],
                    "dp",
                    source,
                ).wait_recv()


def forward_attention(x, weights, cols, rows, biases, gathers):
    n_dp, n_ctx = lax.axis_size("dp"), lax.axis_size("context")
    slab, width = x.shape
    columns = weights[0].shape[1]
    hidden = weights[4].shape[1]
    pairs = columns // PAIR
    groups, share, chunk = slab // CLUSTER, CLUSTER // n_ctx, slab // n_ctx
    vmem = pl.BlockSpec(memory_space=pltpu.VMEM)
    hbm = pl.BlockSpec(memory_space=pl.ANY)
    dma = pltpu.SemaphoreType.DMA
    shapes = (
        jax.ShapeDtypeStruct((slab, width), F32),
        jax.ShapeDtypeStruct((slab, columns), BF16),
        jax.ShapeDtypeStruct((pairs, groups, CLUSTER, 3 * PAIR), BF16),
        jax.ShapeDtypeStruct((width, 4 * columns), BF16),
        jax.ShapeDtypeStruct((width, hidden), BF16),
        jax.ShapeDtypeStruct((width, hidden), BF16),
    )
    weight_spec = hbm if gathers else vmem
    return pl.pallas_call(
        functools.partial(forward_kernel, (n_dp, n_ctx, pairs, gathers)),
        out_shape=shapes,
        in_specs=[vmem] + [weight_spec] * 4 + [hbm] * 2 + [vmem] * 5,
        out_specs=(vmem, vmem, vmem, vmem, hbm, hbm),
        scratch_shapes=[
            pltpu.VMEM((pairs, slab, 3 * PAIR), BF16),
            pltpu.VMEM((pairs, n_ctx, groups, share, 3 * PAIR), BF16),
            pltpu.VMEM((pairs, groups, CLUSTER, PAIR), BF16),
            pltpu.VMEM((pairs, n_ctx, groups, share, PAIR), BF16),
            pltpu.VMEM((slab, width), BF16),
            pltpu.VMEM((slab, width), BF16),
            dma((6,)),
            dma((n_dp,)),
            dma((n_dp, n_ctx)),
            dma((4, n_dp)),
            dma((2, n_dp)),
            dma((2, n_dp)),
            dma((pairs, n_ctx)),
            dma((pairs, n_ctx)),
            dma((pairs, n_ctx)),
            dma((pairs, n_ctx)),
            dma((n_ctx,)),
            dma((n_ctx,)),
        ],
        compiler_params=pltpu.CompilerParams(collective_id=0, has_side_effects=True),
        name="forward_attention",
    )(x, *weights, cols, rows, *biases)


def token_sum(values):
    return jnp.sum(values.astype(F32), axis=0)


def slot_tables(cluster_order, prefix_length, own, n_ctx):
    heads, length = cluster_order.shape[1:]
    slab = length // n_ctx
    order = cluster_order.reshape(heads, n_ctx, slab // CLUSTER, n_ctx, CLUSTER // n_ctx)
    rows = lax.dynamic_index_in_dim(order, own, axis=3, keepdims=False).reshape(heads, slab)
    rows = rows - own * slab
    places = lax.dynamic_slice_in_dim(cluster_order[0], own * slab, slab, axis=1)
    gap = jnp.zeros((8 - heads % 8, slab), jnp.int32)
    limits = jnp.maximum(places, prefix_length[0] - 1)
    along = jnp.concatenate((rows, gap, places, gap), axis=0)
    down = jnp.concatenate((rows, gap, limits, gap), axis=0).T
    return down, along


def permute_rows(values, rows, backward):
    slab = values.shape[1]
    positions = lax.broadcasted_iota(jnp.int32, (1, slab), 1)

    def one_head(pair):
        head_values, head_rows = pair
        table = (head_rows[:, None] == positions).astype(BF16)
        return (dot_tn if backward else dot)(table, head_values).astype(BF16)

    return lax.map(one_head, (values, rows))


def swap(values):
    return lax.all_to_all(values, "context", split_axis=0, concat_axis=0, tiled=True)


def shards(
    tokens,
    prefix_length,
    cluster_order,
    query_weight,
    key_weight,
    value_weight,
    output_weight,
    inner_weight,
    outer_weight,
    query_bias,
    value_bias,
    output_bias,
    inner_bias,
    outer_bias,
    first_gain,
    first_shift,
    second_gain,
    second_shift,
    cotangent,
):
    n_dp, n_ctx = lax.axis_size("dp"), lax.axis_size("context")
    own = lax.axis_index("context")
    x, upstream = tokens[0], cotangent[0].astype(F32)
    slab, width = x.shape
    gathers = query_weight.shape[0] % 16 == 0
    weights = (query_weight, key_weight, value_weight, output_weight.T, inner_weight, outer_weight.T)
    if not gathers:
        weights = tuple(lax.all_gather(w, "dp", axis=0, tiled=True) for w in weights)
    columns = query_weight.shape[1]
    heads = columns // HEAD_DIM
    pairs = heads // 2
    groups, share = slab // CLUSTER, CLUSTER // n_ctx
    cols, rows = slot_tables(cluster_order, prefix_length, own, n_ctx)
    biases = (query_bias[None], value_bias[None], output_bias[None])
    first_in, mixed, got, proj, inner_full, outer_full = forward_attention(
        x, weights, cols, rows, biases, gathers
    )
    if not gathers:
        inner_full, outer_full = weights[4:]
    first_normed, first_root = normalize(first_in)
    first_norm = first_normed * first_gain + first_shift
    first_low = first_norm.astype(BF16)
    inner_pre = dot(first_low, inner_full) + inner_bias
    activated = jax.nn.gelu(inner_pre, approximate=False).astype(BF16)
    feed_part = dot_nt(activated, outer_full)
    feed_out = lax.psum(feed_part.astype(BF16), "tensor").astype(F32) + outer_bias
    second_normed, second_root = normalize(first_norm + feed_out)
    activations = (second_normed * second_gain + second_shift).astype(BF16)
    second_gain_grad = token_sum(upstream * second_normed)
    second_shift_grad = token_sum(upstream)
    second_in_grad = norm_backward(upstream, second_normed, second_root, second_gain)
    feed_grad = second_in_grad.astype(BF16)
    outer_bias_grad = token_sum(feed_grad)
    outer_weight_grad = dot_tn(feed_grad, activated)
    act_grad = dot(feed_grad, outer_full)
    inner_grad = (act_grad * gelu_slope(inner_pre)).astype(BF16)
    inner_bias_grad = token_sum(inner_grad)
    inner_weight_grad = dot_tn(first_low, inner_grad)
    first_part = dot_nt(inner_grad, inner_full)
    first_grad = second_in_grad + lax.psum(first_part.astype(BF16), "tensor").astype(F32)
    first_gain_grad = token_sum(first_grad * first_normed)
    first_shift_grad = token_sum(first_grad)
    summed_grad = norm_backward(first_grad, first_normed, first_root, first_gain)
    branch_grad = summed_grad.astype(BF16)
    output_bias_grad = token_sum(branch_grad)
    output_weight_grad = dot_tn(branch_grad, mixed)
    mixed_grad = dot(branch_grad, proj[:, 3 * columns :]).astype(BF16)

    head_rows = rows[:heads]
    picked = permute_rows(mixed_grad.reshape(slab, heads, HEAD_DIM).transpose(1, 0, 2), head_rows, False)
    picked = picked.reshape(heads, n_ctx, groups, share, HEAD_DIM).transpose(1, 0, 2, 3, 4)
    got_grad = swap(picked).transpose(1, 2, 0, 3, 4).reshape(heads, groups, CLUSTER, HEAD_DIM)
    parts = got.reshape(pairs, groups, CLUSTER, 3, 2, HEAD_DIM).transpose(3, 0, 4, 1, 2, 5)
    query, key, value = parts.reshape(3, heads, groups, CLUSTER, HEAD_DIM)
    allowed = (
        rows[8 : 8 + heads].reshape(heads, groups, 1, CLUSTER)
        <= cols.T[8 : 8 + heads].reshape(heads, groups, CLUSTER, 1)
    )
    scores = jnp.einsum("hcqd,hckd->hcqk", query, key, preferred_element_type=F32)
    scores = jnp.where(allowed, scores * HEAD_DIM ** (-0.5), masked_score)
    probs = jax.nn.softmax(scores, axis=-1)
    prob_grad = jnp.einsum("hcqd,hckd->hcqk", got_grad, value, preferred_element_type=F32)
    value_grad = jnp.einsum(
        "hcqk,hcqd->hckd", probs.astype(BF16), got_grad, preferred_element_type=F32
    ).astype(BF16)
    score_grad = (
        probs
        * (prob_grad - jnp.sum(probs * prob_grad, axis=-1, keepdims=True))
        * HEAD_DIM ** (-0.5)
    ).astype(BF16)
    query_grad = jnp.einsum(
        "hcqk,hckd->hcqd", score_grad, key, preferred_element_type=F32
    ).astype(BF16)
    key_grad = jnp.einsum(
        "hcqk,hcqd->hckd", score_grad, query, preferred_element_type=F32
    ).astype(BF16)
    back = jnp.concatenate((query_grad, key_grad, value_grad), axis=3)
    back = back.reshape(heads, groups, n_ctx, share, 3 * HEAD_DIM).transpose(2, 0, 1, 3, 4)
    back = swap(back).transpose(1, 0, 2, 3, 4).reshape(heads, slab, 3 * HEAD_DIM)
    restored = permute_rows(back, head_rows, True)
    restored = restored.reshape(heads, slab, 3, HEAD_DIM).transpose(1, 2, 0, 3).reshape(slab, 3 * columns)
    bias_sums = token_sum(restored)
    query_bias_grad, value_bias_grad = bias_sums[:columns], bias_sums[2 * columns :]
    proj_weight_grad = dot_tn(x, restored)
    input_part = dot_nt(restored, proj[:, : 3 * columns])
    input_grad = (
        summed_grad + lax.psum(input_part.astype(BF16), "tensor").astype(F32)
    ).astype(BF16)
    small_sums = lax.psum(
        (
            query_bias_grad,
            value_bias_grad,
            output_bias_grad,
            inner_bias_grad,
            outer_bias_grad,
            first_gain_grad,
            first_shift_grad,
            second_gain_grad,
            second_shift_grad,
        ),
        ("dp", "context"),
    )

    def reduced(grad):
        piece = lax.psum_scatter(grad.astype(BF16), "dp", scatter_dimension=0, tiled=True)
        return lax.psum(piece, "context").astype(F32)

    proj_owned = reduced(proj_weight_grad)
    return (
        activations[None],
        input_grad[None],
        proj_owned[:, :columns],
        proj_owned[:, columns : 2 * columns],
        proj_owned[:, 2 * columns :],
        reduced(output_weight_grad).T,
        reduced(inner_weight_grad),
        reduced(outer_weight_grad).T,
        *small_sums,
    )


def solution(mesh):
    placed = (
        P("dp", "context", None),
        P("dp"),
        P("dp", "tensor", None),
        P("dp", "tensor"),
        P("dp", "tensor"),
        P("dp", "tensor"),
        P("tensor", "dp"),
        P("dp", "tensor"),
        P("tensor", "dp"),
        P("tensor"),
        P("tensor"),
        P(),
        P("tensor"),
        P(),
        P(),
        P(),
        P(),
        P(),
        P("dp", "context", None),
    )
    return jax.shard_map(
        shards,
        mesh=mesh,
        in_specs=placed,
        out_specs=(
            P("dp", "context", None),
            P("dp", "context", None),
            P("dp", "tensor"),
            P("dp", "tensor"),
            P("dp", "tensor"),
            P("tensor", "dp"),
            P("dp", "tensor"),
            P("tensor", "dp"),
            P("tensor"),
            P("tensor"),
            P(),
            P("tensor"),
            P(),
            P(),
            P(),
            P(),
            P(),
        ),
        check_vma=False,
    )
```

time: 832 us -> 674 us (0.81)
  Pallas kernels: 0 us -> 116 us
  blocking collectives: 142 us -> 76.2 us
  local copies, waits for them, and re-layouts: 131 us -> 67.3 us
  waiting for transfers between devices: 295 us -> 236 us
  matrix products: 165 us -> 115 us
  starting transfers between devices: 34.8 us -> 9.36 us
    pallas_call x0 -> x1, Pallas kernels: none -> 116 us  [forward_attention(): pl.pallas_call(functools.partial(forward_kernel, (n_dp, n_ctx, pairs, gat...]
    all_gather x4 -> x0, blocking collectives: 65.9 us -> none  [the longest x1 18.6 us: shards(): lax.all_gather(query_weight, 'dp', axis=0, tiled=True)]
    all_gather x2 -> x0, waiting for transfers between devices: 59.1 us -> none  [the longest x1 30.7 us: shards(): lax.all_gather(outer_weight, 'dp', axis=1, tiled=True)]
    dot_general x48 -> x26, matrix products: 165 us -> 111 us  [the longest x9 40.7 us: dot(): lax.dot_general(a, b, (((1,), (0,)), ((), ())), preferred_element_type=F32)]
    reshape x20 -> x2, local copies, waits for them, and re-layouts: 46.6 us -> 2.65 us  [the longest x1 2.44 us: shards(): mixed_grad.reshape(slab, heads, HEAD_DIM).transpose(1, 0, 2)]
    all_to_all x8 -> x2, starting transfers between devices: 33.2 us -> 9.03 us  [swap(): lax.all_to_all(values, 'context', split_axis=0, concat_axis=0, tiled=True)]
    another operation x11 -> x4, local copies, waits for them, and re-layouts: 23.3 us -> 4.93 us  [shards(): query, key, value = parts.reshape(3, heads, groups, CLUSTER, HEAD_DIM)]
    unnamed x16 -> x9, waiting for transfers between devices: 33.9 us -> 16.5 us
  transfers between devices with their start and end apart: 21 -> 10, of which waited for: 13 -> 9; matrix products, arithmetic and copies ran while one was open for 16% -> 7% of each run, Pallas kernels for 0% -> 0%
where the time goes in v1:
time: 674 us; the launch traced here: 664 us
  waiting for transfers between devices  236 us (35%)
  Pallas kernels  116 us (17%)
  matrix products  115 us (17%)
  blocking collectives  76.2 us (11%)
  local copies, waits for them, and re-layouts  67.3 us (10%)
  other arithmetic  28.8 us (4%)
  between operations  15.5 us (2%)
  starting transfers between devices  9.36 us (1%)
    reduce_scatter x3, waiting for transfers between devices, reduced(): lax.psum_scatter(grad.astype(BF16), 'dp', scatter_dimension=0, tiled=True)  119 us
    pallas_call x1, Pallas kernels, forward_attention(): pl.pallas_call(functools.partial(forward_kernel, (n_dp, n_ctx, pairs, gat...  116 us
    psum x1, blocking collectives, shards(): lax.psum((query_bias_grad, value_bias_grad, output_bias_grad, inner_bias_...  76.2 us
    dot_general x9, matrix products, dot(): lax.dot_general(a, b, (((1,), (0,)), ((), ())), preferred_element_type=F32)  40.7 us
    all_to_all x2, waiting for transfers between devices, swap(): lax.all_to_all(values, 'context', split_axis=0, concat_axis=0, tiled=True)  38.7 us
    dot_general x10, matrix products, dot_tn(): lax.dot_general(a, b, (((0,), (0,)), ((), ())), preferred_element_type=F32)  37.6 us
    psum x1, waiting for transfers between devices, shards(): lax.psum(feed_part.astype(BF16), 'tensor').astype(F32) + outer_bias  31.1 us
    unnamed x70, local copies, waits for them, and re-layouts  26.3 us
  transfers between devices with their start and end apart: 10, of which 9 were waited for; matrix products, arithmetic and copies ran while one was open for 7% of the time, Pallas kernels for 0%

profile of v1, /device:TPU:0, one launch (start us, length us, event | category | flops | bytes accessed | tf_op | source)
XLA Modules:
  0.0 663.7 jit_solution(7513077322041074556)
XLA Ops:
  15.7 116.4 %forward_attention.1 = (f32[1024,768]{1,0:T(8,128)}, bf16[1024,384]{1,0:T(8,128)(2,1)}, bf16[3,8,128,384]{3,2,1,0:T(8,128)(2,1)}, bf16[768,1536]{1,0:T(8,128)(2,...) custom-call(bf16[1024,768]{1,0:T(8,128)(2,1)} %bitcast.129, bf16[192,384]{1,0:T(8,128)(2,1)} %query_ref.1, ...), custom_call_target="tpu_custom_call" | custom-call | tf_op jit(solution)/shard_map/forward_attention/pallas_call | solution.py:436
  136.1 17.6 %fusion.24 = (bf16[1024,1536]{1,0:T(8,128)(2,1)S(1)}, f32[1024,1536]{1,0:T(8,128)}) fusion(f32[1536]{0:T(1024)S(1)} %copy-done.26, bf16[768,1536]{1,0:T(8,128)(2,1)S(1)} %copy-done.22, f32[1024,768]{1,0:T(8,128)S(1)} %copy-done, f32[768]{0:T(1024)S(1)} %copy-done.21, f32[768]{0:T(1024)S(1)} %copy-done.17, f32[1024]{0:T(1024)S(1)} %add_rsqrt_fusion.1, ...), kind=kOutput, calls=%fused_computation.28 | convolution fusion | flops 2523660288 | bytes 14962688 | tf_op jit(solution)/shard_map/dot_general | solution.py:42
  159.2 31.1 %all-reduce.7.cloned.1.call-done = bf16[1024,768]{1,0:T(8,128)(2,1)} async-done(((bf16[1024,768]{1,0:T(8,128)(2,1)}), bf16[1024,768]{1,0:T(8,128)(2,1)}) %all-reduce.7.cloned.1.call-update) | async-done | bytes 1572880 | tf_op jit(solution)/shard_map/psum | solution.py:546
  198.2 4.6 convert_reduce_fusion
  208.2 4.3 copy.90
  212.5 17.4 %all-reduce.9.cloned.1.call-done = bf16[1024,768]{1,0:T(8,128)(2,1)} async-done(((bf16[1024,768]{1,0:T(8,128)(2,1)}), bf16[1024,768]{1,0:T(8,128)(2,1)}) %all-reduce.9.cloned.1.call-update) | async-done | bytes 1572880 | tf_op jit(solution)/shard_map/psum | solution.py:560
  229.9 4.8 multiply_reduce_fusion
  243.0 15.7 %while.22 = (s32[]{:T(128)}, bf16[6,1024,64]{1,2,0:T(8,128)(2,1)}, s32[6,1024]{1,0:T(8,128)S(1)}, bf16[6,1024,64]{2,1,0:T(8,128)(2,1)}, s32[]{:T(128)}) while((s32[]{:T(128)}, bf16[6,1024,64]{1,2,0:T(8,128)(2,1)}, s32[6,1024]{1,0:T(8,128)S(1)}, bf16[6,1024,64]{2,1,0:T(8,128)(2,1)}, s32[]{:T(128)}) %tuple.88), condition=%wide.region_13.14_spmd.clone, body=%wide.region_12.13_spmd.clone.sunk | while | flops 135331840 | bytes 406593 | solution.py:493
  268.2 4.4 all-to-all-start
  294.2 6.8 %fusion.74 = bf16[6,8,128,64]{2,3,1,0:T(8,128)(2,1)} fusion(bf16[6,8,128,64]{2,3,1,0:T(8,128)(2,1)} %bitcast.134, f32[6,8,128,128]{2,3,1,0:T(8,128)} %fusion.107, f32[6,8,128,128]{2,3,1,0:T(8,128)} %get-tuple-element.229, f32[6,8,128]{2,1,0:T(8,128)S(1)} %get-tuple-element.228), kind=kOutput, calls=%fused_computation.109 | convolution fusion | flops 106567808 | bytes 7888896 | tf_op jit(solution)/shard_map/hcqk,hckd->hcqd/dot_general | solution.py:591
  301.0 6.7 %fusion.77 = bf16[6,8,128,64]{2,3,1,0:T(8,128)(2,1)} fusion(bf16[6,8,128,64]{2,3,1,0:T(8,128)(2,1)} %bitcast.132, f32[6,8,128,128]{2,3,1,0:T(8,128)} %fusion.107, f32[6,8,128,128]{2,3,1,0:T(8,128)} %get-tuple-element.229, f32[6,8,128]{2,1,0:T(8,128)S(1)} %get-tuple-element.228), kind=kOutput, calls=%fused_computation.110 | convolution fusion | flops 106567808 | bytes 7888896 | tf_op jit(solution)/shard_map/hcqk,hcqd->hckd/dot_general | solution.py:594
  313.0 4.5 copy.103
  321.5 4.7 all-to-all-start.1
  326.2 36.0 %all-to-all-done.1 = bf16[4,6,8,32,192]{4,3,2,1,0:T(8,128)(2,1)} async-done(((bf16[4,6,8,32,192]{4,3,2,1,0:T(8,128)(2,1)}), bf16[4,6,8,32,192]{4,3,2,1,0:T(8,128)(2,1)}, u32[]{:S(2)}, u32[]{:S(2)}) %all-to-all-start.1) | async-done | bytes 2359328 | tf_op jit(solution)/shard_map/all_to_all | solution.py:497
  366.2 17.2 %while.23 = (s32[]{:T(128)}, bf16[6,1024,192]{1,2,0:T(8,128)(2,1)}, s32[6,1024]{1,0:T(8,128)S(1)}, bf16[6,1024,192]{2,1,0:T(8,128)(2,1)}, s32[]{:T(128)}) while((s32[]{:T(128)}, bf16[6,1024,192]{1,2,0:T(8,128)(2,1)}, s32[6,1024]{1,0:T(8,128)S(1)}, bf16[6,1024,192]{2,1,0:T(8,128)(2,1)}, s32[]{:T(128)}) %tuple.89), condition=%wide.region_16.17_spmd.clone, body=%wide.region_15.16_spmd.clone.sunk | while | flops 403898368 | bytes 930881 | solution.py:493
  397.9 6.3 convolution_convert_fusion.1
  404.3 7.0 %convolution_convert_fusion = bf16[768,1536]{1,0:T(8,128)(2,1)} fusion(bf16[1024,1536]{1,0:T(8,128)(2,1)} %copy-done.27, f32[1024,768]{1,0:T(8,128)} %copy-done.3), kind=kOutput, calls=%fused_computation.59 | convolution fusion | flops 2417885184 | bytes 8650752 | tf_op jit(solution)/shard_map/dot_general | solution.py:50
  411.4 4.9 fusion.61
  416.4 16.4 %reduce-scatter.13.cloned.1.call-done = bf16[192,1152]{1,0:T(8,128)(2,1)} async-done(((bf16[768,1152]{1,0:T(8,128)(2,1)}), bf16[192,1152]{1,0:T(8,128)(2,1)}) %reduce-scatter.13.cloned.1.call-update) | async-done | bytes 442384
  434.8 21.8 %reduce-scatter.7.cloned.1.call-done = bf16[192,384]{1,0:T(8,128)(2,1)} async-done(((bf16[768,384]{1,0:T(8,128)(2,1)}), bf16[192,384]{1,0:T(8,128)(2,1)}) %reduce-scatter.7.cloned.1.call-update) | async-done | bytes 147472 | tf_op jit(solution)/shard_map/reduce_scatter | solution.py:625
  456.7 48.3 %reduce-scatter.9.cloned.1.call-done = bf16[192,1536]{1,0:T(8,128)(2,1)} async-done(((bf16[768,1536]{1,0:T(8,128)(2,1)}), bf16[192,1536]{1,0:T(8,128)(2,1)}) %reduce-scatter.9.cloned.1.call-update) | async-done | bytes 589840 | tf_op jit(solution)/shard_map/reduce_scatter | solution.py:625
  505.0 49.3 %reduce-scatter.11.cloned.1.call-done = bf16[192,1536]{1,0:T(8,128)(2,1)} async-done(((bf16[768,1536]{1,0:T(8,128)(2,1)}), bf16[192,1536]{1,0:T(8,128)(2,1)}) %reduce-scatter.11.cloned.1.call-update) | async-done | bytes 589840 | tf_op jit(solution)/shard_map/reduce_scatter | solution.py:625
  558.2 76.2 %all-reduce = (f32[384]{0:T(512)}, f32[384]{0:T(512)}, f32[768]{0:T(1024)}, f32[1536]{0:T(1024)}, f32[768]{0:T(1024)}, /*index=5*/f32[768]{0:T(1024)}, f32[768]{0:T(1024)}, f32[768]{0:T(1024)}, f32[768]{0:T(1024)}) all-reduce(f32[384]{0:T(512)S(1)} %slice.36, ...), channel_id=1, replica_groups=mesh['dp'=4,'context'=4,'tensor'=2] {'dp','context'}, use_global_device_ids=true, to_apply=%region_27.28 | all-reduce | flops 6912 | bytes 55296 | tf_op jit(solution)/shard_map/psum | solution.py:609
  637.3 12.4 %all-reduce.13.cloned.1.call-done = (bf16[192,1152]{0,1:T(8,128)(2,1)}, bf16[384,192]{0,1:T(8,128)(2,1)}, bf16[192,1536]{1,0:T(8,128)(2,1)}, bf16[1536,192]{0,1:T(8,128)(2,1)}) async-done(((bf16[192,1152]{0,1:T(8,128)(2,1)}, bf16[384,192]{0,1:T(8,128)(2,1)}, bf16[192,1536]{1,0:T(8,128)(2,1)}, bf16[1536,192]{0,1:T(8,128)(2,1)}), (bf16[192,1152]{0,1:T(8,128)(2,1)}, bf16[384,192]{0,1:T(8,128)(2,1)}, ...) | async-done | bytes 1769488 | tf_op jit(solution)/shard_map/psum | solution.py:626
  (173 shorter events, 146.3 us)
Async XLA Ops:
  7.2 183.2 %all-reduce.7.cloned.1.call-start = ((), (), s32[]{:S(2)}) async-start(), calls=%async_computation.6 | async-start | bytes 3145728 | tf_op jit(solution)/shard_map/psum | solution.py:546
  136.1 19.3 %copy-start.24 = (bf16[768,1536]{1,0:T(8,128)(2,1)S(1)}, bf16[768,1536]{1,0:T(8,128)(2,1)}, u32[]{:S(2)}) copy-start(bf16[768,1536]{1,0:T(8,128)(2,1)} %get-tuple-element.79) | copy-start | bytes 7077892
  155.4 34.9 %copy-start.19 = (f32[768]{0:T(1024)S(1)}, f32[768]{0:T(1024)}, u32[]{:S(2)}) copy-start(f32[768]{0:T(1024)} %param.36) | copy-start | bytes 9220
  159.2 70.8 %all-reduce.9.cloned.1.call-start = ((), (), s32[]{:S(2)}) async-start(), calls=%async_computation.7 | async-start | bytes 3145728 | tf_op jit(solution)/shard_map/psum | solution.py:560
  190.3 7.8 %slice-start = ((s8[6291456]{0:T(1024)(128)(4,1)}), s8[4194304]{0:T(1024)(128)(4,1)S(1)}, s32[]{:S(2)}) async-start(s8[6291456]{0:T(1024)(128)(4,1)} %bitcast.145), calls=%async_computation.14 | async-start | bytes 8388608
  194.4 3.7 slice-start.1
  198.1 4.6 copy-start.3
  198.2 6.3 copy-start.23
  229.9 4.8 copy-start.4
  229.9 4.8 copy-start.7
  268.2 16.0 %all-to-all-start = ((bf16[4,2,49152]{2,1,0:T(2,128)(2,1)}), bf16[4,2,49152]{2,1,0:T(2,128)(2,1)}, u32[]{:S(2)}, u32[]{:S(2)}) async-start(bf16[4,2,49152]{2,1,0:T(2,128)(2,1)} %reshape.155), calls=%async_computation | async-start | bytes 1572864 | tf_op jit(solution)/shard_map/all_to_all | solution.py:497
  307.7 3.7 copy-start.13
  321.5 40.7 %all-to-all-start.1 = ((bf16[4,6,8,32,192]{4,3,2,1,0:T(8,128)(2,1)}), bf16[4,6,8,32,192]{4,3,2,1,0:T(8,128)(2,1)}, u32[]{:S(2)}, u32[]{:S(2)}) async-start(bf16[4,6,8,32,192]{4,3,2,1,0:T(8,128)(2,1)} %copy.104), calls=%async_computation.1 | async-start | bytes 6291456 | tf_op jit(solution)/shard_map/all_to_all | solution.py:497
  326.1 106.6 %reduce-scatter.13.cloned.1.call-start = ((), (), s32[]{:S(2)}) async-start(), calls=%async_computation.12 | async-start | bytes 2211840
  393.9 62.7 %reduce-scatter.7.cloned.1.call-start = ((), (), s32[]{:S(2)}) async-start(), calls=%async_computation.9 | async-start | bytes 737280 | tf_op jit(solution)/shard_map/reduce_scatter | solution.py:625
  397.9 107.1 %reduce-scatter.9.cloned.1.call-start = ((), (), s32[]{:S(2)}) async-start(), calls=%async_computation.10 | async-start | bytes 2949120 | tf_op jit(solution)/shard_map/reduce_scatter | solution.py:625
  404.3 7.2 %copy-start.10 = (bf16[1024,3,6,64]{0,3,2,1:T(8,128)(2,1)S(1)}, bf16[1024,3,6,64]{0,3,2,1:T(8,128)(2,1)}, u32[]{:S(2)}) copy-start(bf16[1024,3,6,64]{0,3,2,1:T(8,128)(2,1)} %copy-done.9) | copy-start | bytes 7077892
  404.3 150.0 %reduce-scatter.11.cloned.1.call-start = ((), (), s32[]{:S(2)}) async-start(), calls=%async_computation.11 | async-start | bytes 2949120 | tf_op jit(solution)/shard_map/reduce_scatter | solution.py:625
  411.4 222.9 %all-reduce.11.cloned.1.call-start = ((), (), s32[]{:S(2)}) async-start(), calls=%async_computation.8 | async-start | bytes 3145728 | tf_op jit(solution)/shard_map/psum | solution.py:607
  416.4 233.3 %all-reduce.13.cloned.1.call-start = ((), (), s32[]{:S(2)}) async-start(), calls=%async_computation.13 | async-start | bytes 3833856 | tf_op jit(solution)/shard_map/psum | solution.py:626
  434.8 199.5 %copy-start.2 = (f32[1024,768]{1,0:T(8,128)S(1)}, f32[1024,768]{1,0:T(8,128)}, u32[]{:S(2)}) copy-start(f32[1024,768]{1,0:T(8,128)} %copy-done.1) | copy-start | bytes 9437188
  649.7 3.9 copy-start.15
  649.7 5.1 copy-start.14
  651.0 4.9 copy-start.16
  (17 other events, 39.8 us)
Sparse Core Ops, SparseCore 0:
  159.3 31.0 all-reduce.6
  208.3 21.5 all-reduce.8
  394.0 38.6 reduce-scatter.12
  435.5 21.1 reduce-scatter.6
  458.8 46.0 reduce-scatter.8
  507.1 47.0 reduce-scatter.10
  557.1 19.7 all-reduce.10
  581.0 68.6 all-reduce.12

commit v2 on v1

--- a/solution.py
+++ b/solution.py
@@ -25,11 +25,6 @@
     scaled = upstream * gain
     centered = scaled - jnp.mean(scaled, axis=-1, keepdims=True)
     return inverse_root * (centered - normed * jnp.mean(scaled * normed, axis=-1, keepdims=True))
-
-
-def gelu_slope(inner_pre):
-    normal_cdf = 0.5 * (1.0 + lax.erf(inner_pre * 0.7071067811865476))
-    return normal_cdf + inner_pre * jnp.exp(-0.5 * inner_pre * inner_pre) * 0.3989422804014327
 
 
 MESH = pl.DeviceIdType.MESH
@@ -463,8 +458,582 @@
     )(x, *weights, cols, rows, *biases)
 
 
-def token_sum(values):
-    return jnp.sum(values.astype(F32), axis=0)
+def sublane_sums(values):
+    rows, width = values.shape
+    return jnp.sum(values.reshape(rows // 8, 8, width), axis=0)
+
+
+def feed_kernel(
+    blocks,
+    first_in_ref,
+    cotangent_ref,
+    inner_ref,
+    outer_ref,
+    inner_bias_ref,
+    outer_bias_ref,
+    first_gain_ref,
+    first_shift_ref,
+    second_gain_ref,
+    second_shift_ref,
+    activations_ref,
+    summed_ref,
+    branch_ref,
+    inner_grad_ref,
+    outer_grad_ref,
+    sums_ref,
+    low,
+    first,
+    act,
+    slope,
+    feed,
+    part,
+    partner_part,
+    sums,
+    pair_send,
+    pair_recv,
+):
+    slab, width = first_in_ref.shape
+    hidden = inner_ref.shape[1]
+    chunk = slab // blocks
+    core = lax.axis_index("tensor")
+    meet(("tensor",))
+    sums[...] = jnp.zeros_like(sums)
+
+    def rows_of(step):
+        return pl.ds(pl.multiple_of(step * chunk, chunk), chunk)
+
+    def exchange(stage, step):
+        return remote(
+            part.at[stage, rows_of(step)],
+            partner_part.at[stage, rows_of(step)],
+            pair_send.at[stage, step],
+            pair_recv.at[stage, step],
+            "tensor",
+            1 - core,
+        )
+
+    def expand(step, carry):
+        rows = rows_of(step)
+        normed, _ = normalize(first_in_ref[rows, :])
+        values = normed * first_gain_ref[...] + first_shift_ref[...]
+        first[rows, :] = values
+        low[rows, :] = values.astype(BF16)
+        inner = dot(low[rows, :], inner_ref[...]) + inner_bias_ref[...]
+        cdf = 0.5 * (1.0 + lax.erf(inner * 0.7071067811865476))
+        act[rows, :] = (inner * cdf).astype(BF16)
+        slope[rows, :] = (
+            cdf + inner * jnp.exp(-0.5 * inner * inner) * 0.3989422804014327
+        ).astype(BF16)
+        part[0, rows, :] = dot_nt(act[rows, :], outer_ref[...]).astype(BF16)
+        exchange(0, step).start()
+        return carry
+
+    lax.fori_loop(0, blocks, expand, 0)
+
+    def turn(step, carry):
+        rows = rows_of(step)
+        exchange(0, step).wait_recv()
+        out = part[0, rows, :].astype(F32) + partner_part[0, rows, :].astype(F32)
+        normed, root = normalize(first[rows, :] + (out + outer_bias_ref[...]))
+        activations_ref[rows, :] = (
+            normed * second_gain_ref[...] + second_shift_ref[...]
+        ).astype(BF16)
+        upstream = cotangent_ref[rows, :].astype(F32)
+        grad = norm_backward(upstream, normed, root, second_gain_ref[...])
+        first[rows, :] = grad
+        rounded = grad.astype(BF16)
+        feed[rows, :] = rounded
+        sums[2] += sublane_sums(rounded.astype(F32))
+        sums[5] += sublane_sums(upstream * normed)
+        sums[6] += sublane_sums(upstream)
+        inner_grad = dot(rounded, outer_ref[...]) * slope[rows, :].astype(F32)
+        slope[rows, :] = inner_grad.astype(BF16)
+        inner_sums = sublane_sums(slope[rows, :].astype(F32))
+        sums[0] += inner_sums[:, :width]
+        sums[1] += inner_sums[:, width:]
+        part[1, rows, :] = dot_nt(slope[rows, :], inner_ref[...]).astype(BF16)
+        exchange(1, step).start()
+        return carry
+
+    lax.fori_loop(0, blocks, turn, 0)
+
+    strip = hidden // blocks
+
+    def weigh(step, carry):
+        lanes = pl.ds(pl.multiple_of(step * strip, strip), strip)
+        outer_grad_ref[step] = dot_tn(feed[...], act[:, lanes]).astype(BF16)
+        inner_grad_ref[step] = dot_tn(low[...], slope[:, lanes]).astype(BF16)
+        return carry
+
+    lax.fori_loop(0, blocks, weigh, 0)
+
+    def close(step, carry):
+        rows = rows_of(step)
+        exchange(1, step).wait_recv()
+        back = part[1, rows, :].astype(F32) + partner_part[1, rows, :].astype(F32)
+        grad = first[rows, :] + back
+        normed, root = normalize(first_in_ref[rows, :])
+        sums[3] += sublane_sums(grad * normed)
+        sums[4] += sublane_sums(grad)
+        summed = norm_backward(grad, normed, root, first_gain_ref[...])
+        summed_ref[rows, :] = summed
+        rounded = summed.astype(BF16)
+        branch_ref[rows, :] = rounded
+        sums[7] += sublane_sums(rounded.astype(F32))
+        return carry
+
+    lax.fori_loop(0, blocks, close, 0)
+    sums_ref[...] = jnp.sum(sums[...], axis=1)
+
+    def finish(step, carry):
+        exchange(0, step).wait_send()
+        exchange(1, step).wait_send()
+        return carry
+
+    lax.fori_loop(0, blocks, finish, 0)
+
+
+def feed_forward(first_in, cotangent, inner, outer, vectors):
+    slab, width = first_in.shape
+    hidden = inner.shape[1]
+    blocks = lax.axis_size("context")
+    vmem = pl.BlockSpec(memory_space=pltpu.VMEM)
+    dma = pltpu.SemaphoreType.DMA
+    return pl.pallas_call(
+        functools.partial(feed_kernel, blocks),
+        out_shape=(
+            jax.ShapeDtypeStruct((slab, width), BF16),
+            jax.ShapeDtypeStruct((slab, width), F32),
+            jax.ShapeDtypeStruct((slab, width), BF16),
+            jax.ShapeDtypeStruct((blocks, width, hidden // blocks), BF16),
+            jax.ShapeDtypeStruct((blocks, width, hidden // blocks), BF16),
+            jax.ShapeDtypeStruct((8, width), F32),
+        ),
+        in_specs=[vmem] * (4 + len(vectors)),
+        out_specs=[vmem] * 6,
+        scratch_shapes=[
+            pltpu.VMEM((slab, width), BF16),
+            pltpu.VMEM((slab, width), F32),
+            pltpu.VMEM((slab, hidden), BF16),
+            pltpu.VMEM((slab, hidden), BF16),
+            pltpu.VMEM((slab, width), BF16),
+            pltpu.VMEM((2, slab, width), BF16),
+            pltpu.VMEM((2, slab, width), BF16),
+            pltpu.VMEM((8, 8, width), F32),
+            dma((2, blocks)),
+            dma((2, blocks)),
+        ],
+        compiler_params=pltpu.CompilerParams(collective_id=1, has_side_effects=True),
+        name="feed_forward",
+    )(first_in, cotangent, inner, outer, *vectors)
+
+
+def backward_kernel(
+    sizes,
+    x_ref,
+    branch_ref,
+    summed_ref,
+    mixed_ref,
+    got_ref,
+    proj_ref,
+    cols_ref,
+    rows_ref,
+    inner_part_ref,
+    outer_part_ref,
+    sums_ref,
+    input_grad_ref,
+    final_ref,
+    totals_ref,
+    proj_part_ref,
+    upstream,
+    sending,
+    landed,
+    answer,
+    returned,
+    restored,
+    collected,
+    pieces,
+    scattered,
+    part,
+    partner_part,
+    sums,
+    sums_ctx,
+    sums_dp,
+    move_send,
+    move_recv,
+    back_send,
+    back_recv,
+    spread_send,
+    spread_recv,
+    scatter_send,
+    scatter_recv,
+    gather_send,
+    gather_recv,
+    sums_send,
+    sums_recv,
+    pair_send,
+    pair_recv,
+):
+    n_dp, n_ctx, pairs, reduces = sizes
+    slab, width = x_ref.shape
+    columns = pairs * PAIR
+    dp, ctx, core = lax.axis_index("dp"), lax.axis_index("context"), lax.axis_index("tensor")
+    chunk = slab // n_ctx
+    groups = slab // CLUSTER
+    share = CLUSTER // n_ctx
+    shard = width // n_dp
+    meet(("dp", "context", "tensor") if reduces else ("context", "tensor"))
+
+    def rows_of(step):
+        return pl.ds(pl.multiple_of(step * chunk, chunk), chunk)
+
+    def spread(kind, hop):
+        source = (proj_part_ref, inner_part_ref, outer_part_ref)[kind]
+        target = lax.rem(ctx + hop, n_ctx)
+        if hop == 0:
+            return pltpu.make_async_copy(
+                source.at[target], collected.at[kind, 0], spread_recv.at[kind, 0]
+            )
+        return remote(
+            source.at[target],
+            collected.at[kind, hop],
+            spread_send.at[kind, hop],
+            spread_recv.at[kind, hop],
+            "context",
+            target,
+        )
+
+    def scatter(kind, step):
+        target = lax.rem(dp + step, n_dp)
+        rows = pl.ds(pl.multiple_of(target * shard, 16), shard)
+        return remote(
+            pieces.at[kind, rows],
+            scattered.at[kind, step],
+            scatter_send.at[kind, step],
+            scatter_recv.at[kind, step],
+            "dp",
+            target,
+        )
+
+    def regather(kind, hop, mine):
+        owner = ctx if mine else lax.rem(ctx - hop + n_ctx, n_ctx)
+        target = lax.rem(ctx + hop, n_ctx)
+        return remote(
+            final_ref.at[kind, owner],
+            final_ref.at[kind, owner],
+            gather_send.at[kind, hop],
+            gather_recv.at[kind, hop],
+            "context",
+            target,
+        )
+
+    def start_spread(kind):
+        for hop in (*range(1, n_ctx), 0):
+            spread(kind, hop).start()
+
+    def sum_spread(kind):
+        for hop in range(n_ctx):
+            copy = spread(kind, hop)
+            if hop == 0:
+                copy.wait()
+            else:
+                copy.wait_recv()
+
+        def add(step, carry):
+            rows = pl.ds(pl.multiple_of(step * shard, 16), shard)
+            total = collected[kind, 0, rows, :].astype(F32)
+            for hop in range(1, n_ctx):
+                total = total + collected[kind, hop, rows, :].astype(F32)
+            pieces[kind, rows, :] = total.astype(BF16)
+            return carry
+
+        lax.fori_loop(0, n_dp, add, 0)
+        for step in range(1, n_dp):
+            scatter(kind, step).start()
+
+    def sum_scatter(kind):
+        rows = pl.ds(pl.multiple_of(dp * shard, 16), shard)
+        total = pieces[kind, rows, :].astype(F32)
+        for step in range(1, n_dp):
+            scatter(kind, step).wait_recv()
+            total = total + scattered[kind, step].astype(F32)
+        final_ref[kind, ctx] = total.astype(BF16)
+        for hop in range(1, n_ctx):
+            regather(kind, hop, True).start()
+
+    def project(step, carry):
+        rows = rows_of(step)
+        upstream[rows, :] = dot(branch_ref[rows, :], proj_ref[:, 3 * columns :]).astype(BF16)
+        return carry
+
+    lax.fori_loop(0, n_ctx, project, 0)
+
+    own_share = pl.ds(pl.multiple_of(ctx * share, share), share)
+
+    def moved(pair, hop):
+        target = lax.rem(ctx + hop, n_ctx)
+        source = sending.at[pair, target]
+        landing = landed.at[pair, :, own_share, :]
+        if hop == 0:
+            return pltpu.make_async_copy(source, landing, move_recv.at[pair, 0])
+        return remote(
+            source, landing, move_send.at[pair, hop], move_recv.at[pair, hop], "context", target
+        )
+
+    for pair in range(pairs):
+        for hop in (*range(1, n_ctx), 0):
+            target = lax.rem(ctx + hop, n_ctx)
+            rows = rows_of(target)
+            positions = lax.broadcasted_iota(jnp.int32, (chunk, slab), 1)
+            values = upstream[:, pair * PAIR : (pair + 1) * PAIR]
+            even = dot(one_hot(cols_ref[rows, 2 * pair : 2 * pair + 1], positions), values)
+            odd = dot(one_hot(cols_ref[rows, 2 * pair + 1 : 2 * pair + 2], positions), values)
+            picked = jnp.where(low_lanes(even.shape), even, odd).astype(BF16)
+            sending[pair, target] = picked.reshape(groups, share, PAIR)
+            moved(pair, hop).start()
+
+    if reduces:
+        start_spread(2)
+    for step in range(2):
+        rows = slice(step * width // 2, (step + 1) * width // 2)
+        proj_part_ref[3, rows, :] = dot_tn(branch_ref[:, rows], mixed_ref[...]).astype(BF16)
+
+    def sent_back(pair, hop):
+        target = lax.rem(ctx - hop + n_ctx, n_ctx)
+        rows = pl.ds(pl.multiple_of(target * share, share), share)
+        source = answer.at[pair, :, rows, :]
+        landing = returned.at[pair, ctx]
+        if hop == 0:
+            return pltpu.make_async_copy(source, landing, back_recv.at[pair, 0])
+        return remote(
+            source, landing, back_send.at[pair, hop], back_recv.at[pair, hop], "context", target
+        )
+
+    for pair in range(pairs):
+        for hop in range(n_ctx):
+            copy = moved(pair, hop)
+            if hop == 0:
+                copy.wait()
+            else:
+                copy.wait_recv()
+
+        def attend(group, carry):
+            query2 = stack_pair(got_ref[pair, group, :, 0:PAIR])
+            key = got_ref[pair, group, :, PAIR : 2 * PAIR]
+            value = got_ref[pair, group, :, 2 * PAIR : 3 * PAIR]
+            grad2 = stack_pair(landed[pair, group])
+            masks = pair_mask(cols_ref, rows_ref, pair, group, 2 * pairs)
+            raw = dot_nt(query2, key) * HEAD_DIM ** (-0.5)
+            scores = jnp.concatenate(
+                [
+                    jnp.where(mask, raw[i * CLUSTER : (i + 1) * CLUSTER], masked_score)
+                    for i, mask in enumerate(masks)
+                ],
+                axis=0,
+            )
+            exponent = jnp.exp(scores - jnp.max(scores, axis=1, keepdims=True))
+            probs = exponent / jnp.sum(exponent, axis=1, keepdims=True)
+            prob_grad = dot_nt(grad2, value)
+            inner = jnp.sum(probs * prob_grad, axis=1, keepdims=True)
+            score_grad = (probs * (prob_grad - inner) * HEAD_DIM ** (-0.5)).astype(BF16)
+            value_grad = dot_tn(probs.astype(BF16), grad2)
+            query_grad = fold_pair(dot(score_grad, key))
+            key_grad = dot_tn(score_grad, query2)
+            low = low_lanes((CLUSTER, PAIR))
+            first = jnp.where(low, query_grad, pltpu.roll(key_grad, HEAD_DIM, 1))
+            second = jnp.where(low, pltpu.roll(query_grad, HEAD_DIM, 1), key_grad)
+            answer[pair, group, :, 0:PAIR] = first.astype(BF16)
+            answer[pair, group, :, PAIR : 2 * PAIR] = second.astype(BF16)
+            answer[pair, group, :, 2 * PAIR : 3 * PAIR] = value_grad.astype(BF16)
+            return carry
+
+        lax.fori_loop(0, groups, attend, 0, unroll=2)
+        for hop in (*range(1, n_ctx), 0):
+            sent_back(pair, hop).start()
+
+    if reduces:
+        start_spread(1)
+        sum_spread(2)
+    for pair in range(pairs):
+        for hop in range(n_ctx):
+            copy = sent_back(pair, hop)
+            if hop == 0:
+                copy.wait()
+            else:
+                copy.wait_recv()
+
+        def restore(step, carry):
+            rows = rows_of(step)
+            positions = lax.broadcasted_iota(jnp.int32, (chunk, slab), 0) + step * chunk
+            values = returned[pair].reshape(slab, 3 * PAIR)
+            shared = values[:, 2 * PAIR :]
+            even = dot(
+                one_hot(rows_ref[2 * pair : 2 * pair + 1, :], positions),
+                jnp.concatenate((values[:, :PAIR], shared), axis=1),
+            )
+            odd = dot(
+                one_hot(rows_ref[2 * pair + 1 : 2 * pair + 2, :], positions), values[:, PAIR:]
+            )
+            low = low_lanes((chunk, PAIR))
+            first, second = even[:, :PAIR], odd[:, :PAIR]
+            query = jnp.where(low, first, pltpu.roll(second, HEAD_DIM, 1))
+            key = jnp.where(low, pltpu.roll(first, HEAD_DIM, 1), second)
+            value = jnp.where(low, even[:, PAIR:], odd[:, PAIR:])
+            for number, piece in enumerate((query, key, value)):
+                lanes = slice(number * columns + pair * PAIR, number * columns + (pair + 1) * PAIR)
+                restored[rows, lanes] = piece.astype(BF16)
+            return carry
+
+        lax.fori_loop(0, n_ctx, restore, 0)
+
+    for number in range(3):
+        lanes = slice(number * columns, (number + 1) * columns)
+        proj_part_ref[number] = dot_tn(x_ref[...], restored[:, lanes]).astype(BF16)
+    if reduces:
+        start_spread(0)
+
+    def exchange(step):
+        return remote(
+            part.at[rows_of(step)],
+            partner_part.at[rows_of(step)],
+            pair_send.at[step],
+            pair_recv.at[step],
+            "tensor",
+            1 - core,
+        )
+
+    def give(step, carry):
+        rows = rows_of(step)
+        part[rows, :] = dot_nt(restored[rows, :], proj_ref[:, : 3 * columns]).astype(BF16)
+        exchange(step).start()
+        return carry
+
+    lax.fori_loop(0, n_ctx, give, 0)
+
+    sums[0:8, :] = sums_ref[...]
+    sums[8:16, :] = jnp.zeros((8, width), F32)
+    for place, number in enumerate((0, 2)):
+        values = restored[:, number * columns : (number + 1) * columns].astype(F32)
+        sums[8:9, place * columns : (place + 1) * columns] = jnp.sum(values, axis=0, keepdims=True)
+
+    def sums_out(level, step):
+        axis, size, own = (("context", n_ctx, ctx), ("dp", n_dp, dp))[level]
+        landing = (sums_ctx, sums_dp)[level]
+        return remote(
+            sums.at[level * 16 : level * 16 + 16],
+            landing.at[own],
+            sums_send.at[level, step],
+            sums_recv.at[level, step],
+            axis,
+            lax.rem(own + step, size),
+        )
+
+    if reduces:
+        for step in range(1, n_ctx):
+            sums_out(0, step).start()
+        sums_ctx[ctx] = sums[0:16, :]
+
+    def take(step, carry):
+        rows = rows_of(step)
+        exchange(step).wait_recv()
+        back = part[rows, :].astype(F32) + partner_part[rows, :].astype(F32)
+        input_grad_ref[rows, :] = (summed_ref[rows, :] + back).astype(BF16)
+        return carry
+
+    lax.fori_loop(0, n_ctx, take, 0)
+
+    if reduces:
+        sum_scatter(2)
+        for step in range(1, n_ctx):
+            sums_out(0, step).wait_recv()
+        sums[16:32, :] = jnp.sum(sums_ctx[...], axis=0)
+        for step in range(1, n_dp):
+            sums_out(1, step).start()
+        sums_dp[dp] = sums[16:32, :]
+        sum_spread(1)
+        sum_spread(0)
+        for step in range(1, n_dp):
+            sums_out(1, step).wait_recv()
+        totals_ref[...] = jnp.sum(sums_dp[...], axis=0)
+        sum_scatter(1)
+        sum_scatter(0)
+        for kind in range(3):
+            for hop in range(1, n_ctx):
+                regather(kind, hop, False).wait_recv()
+            for hop in range(1, n_ctx):
+                spread(kind, hop).wait_send()
+                regather(kind, hop, True).wait_send()
+            for step in range(1, n_dp):
+                scatter(kind, step).wait_send()
+        for level, size in enumerate((n_ctx, n_dp)):
+            for step in range(1, size):
+                sums_out(level, step).wait_send()
+    else:
+        totals_ref[...] = sums[0:16, :]
+    for step in range(n_ctx):
+        exchange(step).wait_send()
+    for pair in range(pairs):
+        for hop in range(1, n_ctx):
+            moved(pair, hop).wait_send()
+            sent_back(pair, hop).wait_send()
+
+
+def backward_attention(
+    x, branch, summed, mixed, got, proj, cols, rows, inner_part, outer_part, sums, reduces
+):
+    n_dp, n_ctx = lax.axis_size("dp"), lax.axis_size("context")
+    slab, width = x.shape
+    columns = mixed.shape[1]
+    pairs = columns // PAIR
+    groups, share = slab // CLUSTER, CLUSTER // n_ctx
+    shard = width // n_dp
+    vmem = pl.BlockSpec(memory_space=pltpu.VMEM)
+    hbm = pl.BlockSpec(memory_space=pl.ANY)
+    dma = pltpu.SemaphoreType.DMA
+    kinds, steps = (3, n_dp) if reduces else (1, 2)
+    return pl.pallas_call(
+        functools.partial(backward_kernel, (n_dp, n_ctx, pairs, reduces)),
+        out_shape=(
+            jax.ShapeDtypeStruct((slab, width), BF16),
+            jax.ShapeDtypeStruct((kinds, n_ctx, shard, columns), BF16),
+            jax.ShapeDtypeStruct((16, width), F32),
+            jax.ShapeDtypeStruct((4, width, columns), BF16),
+        ),
+        in_specs=[vmem] * 8 + [hbm] * 2 + [vmem],
+        out_specs=[vmem] * 4,
+        scratch_shapes=[
+            pltpu.VMEM((slab, columns), BF16),
+            pltpu.VMEM((pairs, n_ctx, groups, share, PAIR), BF16),
+            pltpu.VMEM((pairs, groups, CLUSTER, PAIR), BF16),
+            pltpu.VMEM((pairs, groups, CLUSTER, 3 * PAIR), BF16),
+            pltpu.VMEM((pairs, n_ctx, groups, share, 3 * PAIR), BF16),
+            pltpu.VMEM((slab, 3 * columns), BF16),
+            pltpu.VMEM((kinds, n_ctx, width, columns), BF16),
+            pltpu.VMEM((kinds, width, columns), BF16),
+            pltpu.VMEM((kinds, steps, shard, columns), BF16),
+            pltpu.VMEM((slab, width), BF16),
+            pltpu.VMEM((slab, width), BF16),
+            pltpu.VMEM((32, width), F32),
+            pltpu.VMEM((n_ctx, 16, width), F32),
+            pltpu.VMEM((steps, 16, width), F32),
+            dma((pairs, n_ctx)),
+            dma((pairs, n_ctx)),
+            dma((pairs, n_ctx)),
+            dma((pairs, n_ctx)),
+            dma((kinds, n_ctx)),
+            dma((kinds, n_ctx)),
+            dma((kinds, steps)),
+            dma((kinds, steps)),
+            dma((kinds, n_ctx)),
+            dma((kinds, n_ctx)),
+            dma((2, max(n_ctx, steps))),
+            dma((2, max(n_ctx, steps))),
+            dma((n_ctx,)),
+            dma((n_ctx,)),
+        ],
+        compiler_params=pltpu.CompilerParams(collective_id=2, has_side_effects=True),
+        name="backward_attention",
+    )(x, branch, summed, mixed, got, proj, cols, rows, inner_part, outer_part, sums)
 
 
 def slot_tables(cluster_order, prefix_length, own, n_ctx):
@@ -479,22 +1048,6 @@
     along = jnp.concatenate((rows, gap, places, gap), axis=0)
     down = jnp.concatenate((rows, gap, limits, gap), axis=0).T
     return down, along
-
-
-def permute_rows(values, rows, backward):
-    slab = values.shape[1]
-    positions = lax.broadcasted_iota(jnp.int32, (1, slab), 1)
-
-    def one_head(pair):
-        head_values, head_rows = pair
-        table = (head_rows[:, None] == positions).astype(BF16)
-        return (dot_tn if backward else dot)(table, head_values).astype(BF16)
-
-    return lax.map(one_head, (values, rows))
-
-
-def swap(values):
-    return lax.all_to_all(values, "context", split_axis=0, concat_axis=0, tiled=True)
 
 
 def shards(
@@ -518,124 +1071,53 @@
     second_shift,
     cotangent,
 ):
-    n_dp, n_ctx = lax.axis_size("dp"), lax.axis_size("context")
+    n_ctx = lax.axis_size("context")
     own = lax.axis_index("context")
-    x, upstream = tokens[0], cotangent[0].astype(F32)
-    slab, width = x.shape
-    gathers = query_weight.shape[0] % 16 == 0
+    x = tokens[0]
+    shard, columns = query_weight.shape
+    aligned = shard % 16 == 0
     weights = (query_weight, key_weight, value_weight, output_weight.T, inner_weight, outer_weight.T)
-    if not gathers:
+    if not aligned:
         weights = tuple(lax.all_gather(w, "dp", axis=0, tiled=True) for w in weights)
-    columns = query_weight.shape[1]
-    heads = columns // HEAD_DIM
-    pairs = heads // 2
-    groups, share = slab // CLUSTER, CLUSTER // n_ctx
     cols, rows = slot_tables(cluster_order, prefix_length, own, n_ctx)
     biases = (query_bias[None], value_bias[None], output_bias[None])
     first_in, mixed, got, proj, inner_full, outer_full = forward_attention(
-        x, weights, cols, rows, biases, gathers
+        x, weights, cols, rows, biases, aligned
     )
-    if not gathers:
+    if not aligned:
         inner_full, outer_full = weights[4:]
-    first_normed, first_root = normalize(first_in)
-    first_norm = first_normed * first_gain + first_shift
-    first_low = first_norm.astype(BF16)
-    inner_pre = dot(first_low, inner_full) + inner_bias
-    activated = jax.nn.gelu(inner_pre, approximate=False).astype(BF16)
-    feed_part = dot_nt(activated, outer_full)
-    feed_out = lax.psum(feed_part.astype(BF16), "tensor").astype(F32) + outer_bias
-    second_normed, second_root = normalize(first_norm + feed_out)
-    activations = (second_normed * second_gain + second_shift).astype(BF16)
-    second_gain_grad = token_sum(upstream * second_normed)
-    second_shift_grad = token_sum(upstream)
-    second_in_grad = norm_backward(upstream, second_normed, second_root, second_gain)
-    feed_grad = second_in_grad.astype(BF16)
-    outer_bias_grad = token_sum(feed_grad)
-    outer_weight_grad = dot_tn(feed_grad, activated)
-    act_grad = dot(feed_grad, outer_full)
-    inner_grad = (act_grad * gelu_slope(inner_pre)).astype(BF16)
-    inner_bias_grad = token_sum(inner_grad)
-    inner_weight_grad = dot_tn(first_low, inner_grad)
-    first_part = dot_nt(inner_grad, inner_full)
-    first_grad = second_in_grad + lax.psum(first_part.astype(BF16), "tensor").astype(F32)
-    first_gain_grad = token_sum(first_grad * first_normed)
-    first_shift_grad = token_sum(first_grad)
-    summed_grad = norm_backward(first_grad, first_normed, first_root, first_gain)
-    branch_grad = summed_grad.astype(BF16)
-    output_bias_grad = token_sum(branch_grad)
-    output_weight_grad = dot_tn(branch_grad, mixed)
-    mixed_grad = dot(branch_grad, proj[:, 3 * columns :]).astype(BF16)
-
-    head_rows = rows[:heads]
-    picked = permute_rows(mixed_grad.reshape(slab, heads, HEAD_DIM).transpose(1, 0, 2), head_rows, False)
-    picked = picked.reshape(heads, n_ctx, groups, share, HEAD_DIM).transpose(1, 0, 2, 3, 4)
-    got_grad = swap(picked).transpose(1, 2, 0, 3, 4).reshape(heads, groups, CLUSTER, HEAD_DIM)
-    parts = got.reshape(pairs, groups, CLUSTER, 3, 2, HEAD_DIM).transpose(3, 0, 4, 1, 2, 5)
-    query, key, value = parts.reshape(3, heads, groups, CLUSTER, HEAD_DIM)
-    allowed = (
-        rows[8 : 8 + heads].reshape(heads, groups, 1, CLUSTER)
-        <= cols.T[8 : 8 + heads].reshape(heads, groups, CLUSTER, 1)
+    vectors = (inner_bias, outer_bias, first_gain, first_shift, second_gain, second_shift)
+    activations, summed, branch, inner_part, outer_part, sums = feed_forward(
+        first_in, cotangent[0], inner_full, outer_full, tuple(v[None] for v in vectors)
     )
-    scores = jnp.einsum("hcqd,hckd->hcqk", query, key, preferred_element_type=F32)
-    scores = jnp.where(allowed, scores * HEAD_DIM ** (-0.5), masked_score)
-    probs = jax.nn.softmax(scores, axis=-1)
-    prob_grad = jnp.einsum("hcqd,hckd->hcqk", got_grad, value, preferred_element_type=F32)
-    value_grad = jnp.einsum(
-        "hcqk,hcqd->hckd", probs.astype(BF16), got_grad, preferred_element_type=F32
-    ).astype(BF16)
-    score_grad = (
-        probs
-        * (prob_grad - jnp.sum(probs * prob_grad, axis=-1, keepdims=True))
-        * HEAD_DIM ** (-0.5)
-    ).astype(BF16)
-    query_grad = jnp.einsum(
-        "hcqk,hckd->hcqd", score_grad, key, preferred_element_type=F32
-    ).astype(BF16)
-    key_grad = jnp.einsum(
-        "hcqk,hcqd->hckd", score_grad, query, preferred_element_type=F32
-    ).astype(BF16)
-    back = jnp.concatenate((query_grad, key_grad, value_grad), axis=3)
-    back = back.reshape(heads, groups, n_ctx, share, 3 * HEAD_DIM).transpose(2, 0, 1, 3, 4)
-    back = swap(back).transpose(1, 0, 2, 3, 4).reshape(heads, slab, 3 * HEAD_DIM)
-    restored = permute_rows(back, head_rows, True)
-    restored = restored.reshape(heads, slab, 3, HEAD_DIM).transpose(1, 2, 0, 3).reshape(slab, 3 * columns)
-    bias_sums = token_sum(restored)
-    query_bias_grad, value_bias_grad = bias_sums[:columns], bias_sums[2 * columns :]
-    proj_weight_grad = dot_tn(x, restored)
-    input_part = dot_nt(restored, proj[:, : 3 * columns])
-    input_grad = (
-        summed_grad + lax.psum(input_part.astype(BF16), "tensor").astype(F32)
-    ).astype(BF16)
-    small_sums = lax.psum(
-        (
-            query_bias_grad,
-            value_bias_grad,
-            output_bias_grad,
-            inner_bias_grad,
-            outer_bias_grad,
-            first_gain_grad,
-            first_shift_grad,
-            second_gain_grad,
-            second_shift_grad,
-        ),
-        ("dp", "context"),
+    input_grad, final, totals, proj_part = backward_attention(
+        x, branch, summed, mixed, got, proj, cols, rows, inner_part, outer_part, sums, aligned
     )
-
-    def reduced(grad):
-        piece = lax.psum_scatter(grad.astype(BF16), "dp", scatter_dimension=0, tiled=True)
-        return lax.psum(piece, "context").astype(F32)
-
-    proj_owned = reduced(proj_weight_grad)
+    if not aligned:
+        parts = jnp.stack((proj_part, inner_part, outer_part))
+        piece = lax.psum_scatter(parts, "dp", scatter_dimension=2, tiled=True)
+        final = lax.psum(piece, "context")
+        totals = lax.psum(totals, ("dp", "context"))
+    final = final.astype(F32)
+    wide = final.transpose(0, 2, 1, 3).reshape(3, shard, n_ctx * columns)
     return (
         activations[None],
         input_grad[None],
-        proj_owned[:, :columns],
-        proj_owned[:, columns : 2 * columns],
-        proj_owned[:, 2 * columns :],
-        reduced(output_weight_grad).T,
-        reduced(inner_weight_grad),
-        reduced(outer_weight_grad).T,
-        *small_sums,
+        final[0, 0],
+        final[0, 1],
+        final[0, 2],
+        final[0, 3].T,
+        wide[1],
+        wide[2].T,
+        totals[8, :columns],
+        totals[8, columns:],
+        totals[7],
+        totals[0:2].reshape(-1),
+        totals[2],
+        totals[3],
+        totals[4],
+        totals[5],
+        totals[6],
     )
 
 

time: 674 us -> 358 us (0.53); the launches traced: 664 us -> 356 us
  waiting for transfers between devices: 236 us -> 0 us
  Pallas kernels: 116 us -> 325 us
  matrix products: 115 us -> 0 us
  blocking collectives: 76.2 us -> 0 us
  local copies, waits for them, and re-layouts: 67.3 us -> 25.8 us
  other arithmetic: 28.8 us -> 4.06 us
  between operations: 15.5 us -> 1.41 us
  starting transfers between devices: 9.36 us -> 0 us
    pallas_call x0 -> x2, Pallas kernels: none -> 208 us  [the longest x1 173 us: backward_attention(): pl.pallas_call(functools.partial(backward_kernel, (n_dp, n_ctx, pairs, re...]
    reduce_scatter x3 -> x0, waiting for transfers between devices: 119 us -> none  [reduced(): lax.psum_scatter(grad.astype(BF16), 'dp', scatter_dimension=0, tiled=True)]
    dot_general x26 -> x0, matrix products: 111 us -> none  [the longest x9 40.7 us: dot(): lax.dot_general(a, b, (((1,), (0,)), ((), ())), preferred_element_type=F32)]
    psum x1 -> x0, blocking collectives: 76.2 us -> none  [shards(): lax.psum((query_bias_grad, value_bias_grad, output_bias_grad, inner_bias_...]
    psum x4 -> x0, waiting for transfers between devices: 61 us -> none  [the longest x1 31.1 us: shards(): lax.psum(feed_part.astype(BF16), 'tensor').astype(F32) + outer_bias]
    all_to_all x2 -> x0, waiting for transfers between devices: 38.7 us -> none  [swap(): lax.all_to_all(values, 'context', split_axis=0, concat_axis=0, tiled=True)]
    unnamed x70 -> x9, local copies, waits for them, and re-layouts: 26.3 us -> 5.29 us
    reduce_sum x9 -> x0, other arithmetic: 17.1 us -> none  [the longest x5 11.3 us: token_sum(): return jnp.sum(values.astype(F32), axis=0)]
  transfers between devices with their start and end apart: 10 -> 0, of which waited for: 9 -> 0; matrix products, arithmetic and copies ran while one was open for 7% -> 0% of each run, Pallas kernels for 0% -> 0%
where the time goes in v2:
time: 358 us; the launch traced here: 356 us
  Pallas kernels  325 us (91%)
  local copies, waits for them, and re-layouts  25.8 us (7%)
  other arithmetic  4.06 us (1%)
    pallas_call x1, Pallas kernels, backward_attention(): pl.pallas_call(functools.partial(backward_kernel, (n_dp, n_ctx, pairs, re...  173 us
    pallas_call x1, Pallas kernels, forward_attention(): pl.pallas_call(functools.partial(forward_kernel, (n_dp, n_ctx, pairs, gat...  117 us
    pallas_call x1, Pallas kernels, feed_forward(): pl.pallas_call(functools.partial(feed_kernel, blocks), out_shape=(jax.Sha...  35.2 us
    broadcast_in_dim x6, local copies, waits for them, and re-layouts, shards(): v[None]  7.63 us

profile of v2, /device:TPU:0, one launch (start us, length us, event | category | flops | bytes accessed | tf_op | source)
XLA Modules:
  0.0 356.1 jit_solution(7375799843019351274)
XLA Ops:
  1.3 1.2 broadcast_in_dim.37.query_bias_ref
  2.6 1.2 broadcast_in_dim.38.value_bias_ref
  3.8 1.3 broadcast_in_dim.39.output_bias_ref
  5.1 1.3 broadcast_in_dim.41.outer_bias_ref
  6.3 1.3 broadcast_in_dim.42.first_gain_ref
  7.6 1.3 broadcast_in_dim.43.first_shift_ref
  8.9 1.3 broadcast_in_dim.44.second_gain_ref
  10.1 1.3 broadcast_in_dim.45.second_shift_ref
  11.4 1.3 broadcast_in_dim.40.inner_bias_ref
  13.5 1.1 reduce
  15.7 1.0 copy.40.cols_ref
  16.7 116.5 %forward_attention.1 = (f32[1024,768]{1,0:T(8,128)}, bf16[1024,384]{1,0:T(8,128)(2,1)}, bf16[3,8,128,384]{3,2,1,0:T(8,128)(2,1)}, bf16[768,1536]{1,0:T(8,128)(2,...) custom-call(bf16[1024,768]{1,0:T(8,128)(2,1)} %bitcast.39, bf16[192,384]{1,0:T(8,128)(2,1)} %query_ref.1, ...), custom_call_target="tpu_custom_call" | custom-call | tf_op jit(solution)/shard_map/forward_attention/pallas_call | solution.py:431
  133.2 35.2 %feed_forward.1 = (bf16[1024,768]{1,0:T(8,128)(2,1)}, f32[1024,768]{1,0:T(8,128)}, bf16[1024,768]{1,0:T(8,128)(2,1)}, bf16[4,768,384]{2,1,0:T(8,128)(2,1)}, bf16...) custom-call(f32[1024,768]{1,0:T(8,128)} %get-tuple-element.32.first_in_ref, bf16[1024,768]{1,0:T(8,128)(2,1)} %bitcast.43, ...), custom_call_target="tpu_custom_call" | custom-call | tf_op jit(solution)/shard_map/feed_forward/pallas_call | solution.py:602
  168.4 173.1 %backward_attention.1 = (bf16[1024,768]{1,0:T(8,128)(2,1)}, bf16[3,4,192,384]{3,2,1,0:T(8,128)(2,1)}, f32[16,768]{1,0:T(8,128)}, bf16[4,768,384]{2,1,0:T(8,128)(2,1)}) custom-call(bf16[1024,768]{1,0:T(8,128)(2,1)} %bitcast.40, bf16[1024,768]{1,0:T(8,128)(2,1)} %get-tuple-element.36.branch_ref, f32[1024,768]{1,0:T(8,128)} %get-tuple-element.37.summed_ref, ...), custom_call_target="tpu_custom_call" | custom-call | tf_op jit(solution)/shard_map/backward_attention/pallas_call | solution.py:994
  341.6 1.3 slice_reduce_fusion.6
  343.6 1.6 slice_reduce_fusion
  345.9 2.3 convert_bitcast_fusion
  348.3 0.8 copy.43
  349.1 1.1 copy.47
  350.9 1.1 copy.46
  352.0 1.0 slice_bitcast_fusion
  353.1 0.8 copy-done
  353.9 1.1 copy.55
  355.0 1.1 copy.56
  (16 shorter events, 4.1 us)
Async XLA Ops:
  352.0 1.8 copy-start
  353.0 2.0 copy-start.1

commit v3 on v2

--- a/solution.py
+++ b/solution.py
@@ -70,6 +70,10 @@
             )
             count += 1
     pl.semaphore_wait(barrier, count)
+
+
+def row_of(ref):
+    return ref[...].reshape(1, ref.shape[0])
 
 
 def low_lanes(shape):
@@ -139,6 +143,9 @@
     gather_recv,
     feed_send,
     feed_recv,
+    inner_send,
+    inner_forward,
+    inner_recv,
     move_send,
     move_recv,
     back_send,
@@ -192,20 +199,58 @@
             )
             copy.start()
             gather_copies.append(copy)
-        for number, (source, full) in enumerate(
-            ((inner_ref, inner_full_ref), (outer_ref, outer_full_ref))
-        ):
-            for step in range(1, n_dp):
+
+        def strip(rows_of, block_number):
+            rows = pl.ds(pl.multiple_of(rows_of * shard, 16), shard)
+            lanes = pl.ds(pl.multiple_of(block_number * columns, columns), columns)
+            return inner_full_ref.at[rows, lanes]
+
+        own_lanes = pl.ds(pl.multiple_of(ctx * columns, columns), columns)
+        for step in range(1, n_dp):
+            copy = remote(
+                inner_ref.at[:, own_lanes],
+                strip(dp, ctx),
+                inner_send.at[step],
+                inner_recv.at[ctx, dp],
+                "dp",
+                lax.rem(dp + step, n_dp),
+            )
+            copy.start()
+            feed_copies.append(copy)
+        for step in range(1, n_dp):
+            copy = remote(
+                outer_ref,
+                outer_full_ref.at[own_rows],
+                feed_send.at[step],
+                feed_recv.at[dp],
+                "dp",
+                lax.rem(dp + step, n_dp),
+            )
+            copy.start()
+            feed_copies.append(copy)
+
+        def forward_strip(step):
+            source = lax.rem(dp - step + n_dp, n_dp)
+            remote(
+                strip(source, ctx),
+                strip(source, ctx),
+                inner_send.at[step],
+                inner_recv.at[ctx, source],
+                "dp",
+                source,
+            ).wait_recv()
+            for hop in range(1, n_ctx):
                 copy = remote(
-                    source,
-                    full.at[own_rows],
-                    feed_send.at[number, step],
-                    feed_recv.at[number, dp],
-                    "dp",
-                    lax.rem(dp + step, n_dp),
+                    strip(source, ctx),
+                    strip(source, ctx),
+                    inner_forward.at[step, hop],
+                    inner_recv.at[ctx, source],
+                    "context",
+                    lax.rem(ctx + hop, n_ctx),
                 )
                 copy.start()
                 feed_copies.append(copy)
+
         for step in range(1, n_dp):
             source = lax.rem(dp - step + n_dp, n_dp)
             remote(
@@ -243,17 +288,20 @@
         for number, source in enumerate((query_ref, key_ref, value_ref, output_ref)):
             proj_ref[:, number * columns : (number + 1) * columns] = source[...]
 
+    query_bias, value_bias = row_of(query_bias_ref), row_of(value_bias_ref)
+    output_bias = row_of(output_bias_ref)
+
     def project(step, carry):
         rows = pl.ds(pl.multiple_of(step * chunk, chunk), chunk)
         values = dot(x_ref[rows, :], proj_ref[:, : 3 * columns])
         low = low_lanes((chunk, PAIR))
         for pair in range(pairs):
             lanes = slice(pair * PAIR, (pair + 1) * PAIR)
-            query = values[:, lanes] + query_bias_ref[:, lanes]
+            query = values[:, lanes] + query_bias[:, lanes]
             key = values[:, columns + pair * PAIR : columns + (pair + 1) * PAIR]
             value = (
                 values[:, 2 * columns + pair * PAIR : 2 * columns + (pair + 1) * PAIR]
-                + value_bias_ref[:, lanes]
+                + value_bias[:, lanes]
             )
             first = jnp.where(low, query, pltpu.roll(key, HEAD_DIM, 1))
             second = jnp.where(low, pltpu.roll(query, HEAD_DIM, 1), key)
@@ -262,6 +310,8 @@
             packed[pair, rows, 2 * PAIR : 3 * PAIR] = value.astype(BF16)
         return carry
 
+    if gathers:
+        forward_strip(1)
     lax.fori_loop(0, n_ctx, project, 0)
 
     own_share = pl.ds(pl.multiple_of(ctx * share, share), share)
@@ -340,6 +390,9 @@
         lax.fori_loop(0, groups, attend, 0, unroll=2)
         for hop in (*range(1, n_ctx), 0):
             sent_back(pair, hop).start()
+    if gathers:
+        for step in range(2, n_dp):
+            forward_strip(step)
 
     for pair in range(pairs):
         for hop in range(n_ctx):
@@ -381,7 +434,7 @@
         rows = slice(step * chunk, (step + 1) * chunk)
         exchange(step).wait_recv()
         branch = part[rows, :].astype(F32) + partner_part[rows, :].astype(F32)
-        first_in_ref[rows, :] = x_ref[rows, :].astype(F32) + (branch + output_bias_ref[...])
+        first_in_ref[rows, :] = x_ref[rows, :].astype(F32) + (branch + output_bias)
 
     for step in range(n_ctx):
         exchange(step).wait_send()
@@ -394,18 +447,28 @@
             copy.wait_send()
         for copy in feed_copies:
             copy.wait_send()
-        for number, full in enumerate((inner_full_ref, outer_full_ref)):
-            own[4 + number].wait()
-            for step in range(1, n_dp):
-                source = lax.rem(dp - step + n_dp, n_dp)
-                rows = pl.ds(pl.multiple_of(source * shard, 16), shard)
+        own[4].wait()
+        own[5].wait()
+        for step in range(1, n_dp):
+            source = lax.rem(dp - step + n_dp, n_dp)
+            rows = pl.ds(pl.multiple_of(source * shard, 16), shard)
+            remote(
+                outer_full_ref.at[rows],
+                outer_full_ref.at[rows],
+                feed_send.at[step],
+                feed_recv.at[source],
+                "dp",
+                source,
+            ).wait_recv()
+            for hop in range(1, n_ctx):
+                other = lax.rem(ctx - hop + n_ctx, n_ctx)
                 remote(
-                    full.at[rows],
-                    full.at[rows],
-                    feed_send.at[number, step],
-                    feed_recv.at[number, source],
-                    "dp",
-                    source,
+                    strip(source, other),
+                    strip(source, other),
+                    inner_forward.at[step, hop],
+                    inner_recv.at[other, source],
+                    "context",
+                    other,
                 ).wait_recv()
 
 
@@ -444,8 +507,11 @@
             dma((n_dp,)),
             dma((n_dp, n_ctx)),
             dma((4, n_dp)),
-            dma((2, n_dp)),
-            dma((2, n_dp)),
+            dma((n_dp,)),
+            dma((n_dp,)),
+            dma((n_dp,)),
+            dma((n_dp, n_ctx)),
+            dma((n_ctx, n_dp)),
             dma((pairs, n_ctx)),
             dma((pairs, n_ctx)),
             dma((pairs, n_ctx)),
@@ -456,6 +522,24 @@
         compiler_params=pltpu.CompilerParams(collective_id=0, has_side_effects=True),
         name="forward_attention",
     )(x, *weights, cols, rows, *biases)
+
+
+def store_chunk(ref, index, values):
+    if len(ref.shape) == 3:
+        ref[index] = values
+        return
+    n_ctx, n_dp, tile = ref.shape[1:4]
+    for owner in range(n_dp):
+        for place in range(n_ctx):
+            row = (owner * n_ctx + place) * tile
+            ref[index, place, owner] = values[row : row + tile]
+
+
+def chunk_shape(count, width, columns, split):
+    n_dp, n_ctx = lax.axis_size("dp"), lax.axis_size("context")
+    if split:
+        return (count, n_ctx, n_dp, width // (n_dp * n_ctx), columns)
+    return (count, width, columns)
 
 
 def sublane_sums(values):
@@ -497,6 +581,9 @@
     chunk = slab // blocks
     core = lax.axis_index("tensor")
     meet(("tensor",))
+    inner_bias, outer_bias = row_of(inner_bias_ref), row_of(outer_bias_ref)
+    first_gain, first_shift = row_of(first_gain_ref), row_of(first_shift_ref)
+    second_gain, second_shift = row_of(second_gain_ref), row_of(second_shift_ref)
     sums[...] = jnp.zeros_like(sums)
 
     def rows_of(step):
@@ -515,10 +602,10 @@
     def expand(step, carry):
         rows = rows_of(step)
         normed, _ = normalize(first_in_ref[rows, :])
-        values = normed * first_gain_ref[...] + first_shift_ref[...]
+        values = normed * first_gain + first_shift
         first[rows, :] = values
         low[rows, :] = values.astype(BF16)
-        inner = dot(low[rows, :], inner_ref[...]) + inner_bias_ref[...]
+        inner = dot(low[rows, :], inner_ref[...]) + inner_bias
         cdf = 0.5 * (1.0 + lax.erf(inner * 0.7071067811865476))
         act[rows, :] = (inner * cdf).astype(BF16)
         slope[rows, :] = (
@@ -534,12 +621,12 @@
         rows = rows_of(step)
         exchange(0, step).wait_recv()
         out = part[0, rows, :].astype(F32) + partner_part[0, rows, :].astype(F32)
-        normed, root = normalize(first[rows, :] + (out + outer_bias_ref[...]))
+        normed, root = normalize(first[rows, :] + (out + outer_bias))
         activations_ref[rows, :] = (
-            normed * second_gain_ref[...] + second_shift_ref[...]
+            normed * second_gain + second_shift
         ).astype(BF16)
         upstream = cotangent_ref[rows, :].astype(F32)
-        grad = norm_backward(upstream, normed, root, second_gain_ref[...])
+        grad = norm_backward(upstream, normed, root, second_gain)
         first[rows, :] = grad
         rounded = grad.astype(BF16)
         feed[rows, :] = rounded
@@ -561,8 +648,8 @@
 
     def weigh(step, carry):
         lanes = pl.ds(pl.multiple_of(step * strip, strip), strip)
-        outer_grad_ref[step] = dot_tn(feed[...], act[:, lanes]).astype(BF16)
-        inner_grad_ref[step] = dot_tn(low[...], slope[:, lanes]).astype(BF16)
+        store_chunk(outer_grad_ref, step, dot_tn(feed[...], act[:, lanes]).astype(BF16))
+        store_chunk(inner_grad_ref, step, dot_tn(low[...], slope[:, lanes]).astype(BF16))
         return carry
 
     lax.fori_loop(0, blocks, weigh, 0)
@@ -575,7 +662,7 @@
         normed, root = normalize(first_in_ref[rows, :])
         sums[3] += sublane_sums(grad * normed)
         sums[4] += sublane_sums(grad)
-        summed = norm_backward(grad, normed, root, first_gain_ref[...])
+        summed = norm_backward(grad, normed, root, first_gain)
         summed_ref[rows, :] = summed
         rounded = summed.astype(BF16)
         branch_ref[rows, :] = rounded
@@ -593,7 +680,7 @@
     lax.fori_loop(0, blocks, finish, 0)
 
 
-def feed_forward(first_in, cotangent, inner, outer, vectors):
+def feed_forward(first_in, cotangent, inner, outer, vectors, split):
     slab, width = first_in.shape
     hidden = inner.shape[1]
     blocks = lax.axis_size("context")
@@ -605,8 +692,8 @@
             jax.ShapeDtypeStruct((slab, width), BF16),
             jax.ShapeDtypeStruct((slab, width), F32),
             jax.ShapeDtypeStruct((slab, width), BF16),
-            jax.ShapeDtypeStruct((blocks, width, hidden // blocks), BF16),
-            jax.ShapeDtypeStruct((blocks, width, hidden // blocks), BF16),
+            jax.ShapeDtypeStruct(chunk_shape(blocks, width, hidden // blocks, split), BF16),
+            jax.ShapeDtypeStruct(chunk_shape(blocks, width, hidden // blocks, split), BF16),
             jax.ShapeDtypeStruct((8, width), F32),
         ),
         in_specs=[vmem] * (4 + len(vectors)),
@@ -653,7 +740,7 @@
     restored,
     collected,
     pieces,
-    scattered,
+    gathered,
     part,
     partner_part,
     sums,
@@ -663,12 +750,12 @@
     move_recv,
     back_send,
     back_recv,
-    spread_send,
-    spread_recv,
-    scatter_send,
-    scatter_recv,
-    gather_send,
-    gather_recv,
+    first_send,
+    first_recv,
+    second_send,
+    second_recv,
+    third_send,
+    third_recv,
     sums_send,
     sums_recv,
     pair_send,
@@ -687,79 +774,100 @@
     def rows_of(step):
         return pl.ds(pl.multiple_of(step * chunk, chunk), chunk)
 
-    def spread(kind, hop):
-        source = (proj_part_ref, inner_part_ref, outer_part_ref)[kind]
-        target = lax.rem(ctx + hop, n_ctx)
+    strips = n_ctx
+    half = strips // 2
+    groups_of = [(proj_part_ref, number, 1, number, "context") for number in range(1 + pairs)]
+    inner_near, inner_far, outer_far = range(1 + pairs, 4 + pairs)
+    groups_of.append((inner_part_ref, 0, half, 1 + pairs, "context"))
+    groups_of.append((inner_part_ref, half, strips - half, 1 + pairs + half, "dp"))
+    groups_of.append((outer_part_ref, 0, strips, 1 + pairs + strips, "dp"))
+    places = {"context": (n_ctx, ctx, "dp"), "dp": (n_dp, dp, "context")}
+
+    def first(group, hop):
+        source, start, count, chunk, axis = groups_of[group]
+        size, own, _ = places[axis]
+        target = lax.rem(own + hop, size)
+        if axis == "context":
+            sent = source.at[start : start + count, target]
+        else:
+            sent = source.at[start : start + count, :, target]
+        landing = collected.at[hop, chunk : chunk + count]
         if hop == 0:
-            return pltpu.make_async_copy(
-                source.at[target], collected.at[kind, 0], spread_recv.at[kind, 0]
-            )
+            return pltpu.make_async_copy(sent, landing, first_recv.at[group, 0])
         return remote(
-            source.at[target],
-            collected.at[kind, hop],
-            spread_send.at[kind, hop],
-            spread_recv.at[kind, hop],
-            "context",
+            sent, landing, first_send.at[group, hop], first_recv.at[group, hop], axis, target
+        )
+
+    def second(group, hop):
+        _, _, count, chunk, axis = groups_of[group]
+        other = places[axis][2]
+        size, own, _ = places[other]
+        target = lax.rem(own + hop, size)
+        return remote(
+            pieces.at[chunk : chunk + count, target],
+            gathered.at[hop, chunk : chunk + count],
+            second_send.at[group, hop],
+            second_recv.at[group, hop],
+            other,
             target,
         )
 
-    def scatter(kind, step):
-        target = lax.rem(dp + step, n_dp)
-        rows = pl.ds(pl.multiple_of(target * shard, 16), shard)
+    def third(group, hop, mine):
+        _, _, count, chunk, _ = groups_of[group]
+        owner = ctx if mine else lax.rem(ctx - hop + n_ctx, n_ctx)
+        block = final_ref.at[chunk : chunk + count, owner]
         return remote(
-            pieces.at[kind, rows],
-            scattered.at[kind, step],
-            scatter_send.at[kind, step],
-            scatter_recv.at[kind, step],
-            "dp",
-            target,
+            block,
+            block,
+            third_send.at[group, hop],
+            third_recv.at[group, hop],
+            "context",
+            lax.rem(ctx + hop, n_ctx),
         )
 
-    def regather(kind, hop, mine):
-        owner = ctx if mine else lax.rem(ctx - hop + n_ctx, n_ctx)
-        target = lax.rem(ctx + hop, n_ctx)
-        return remote(
-            final_ref.at[kind, owner],
-            final_ref.at[kind, owner],
-            gather_send.at[kind, hop],
-            gather_recv.at[kind, hop],
-            "context",
-            target,
-        )
-
-    def start_spread(kind):
-        for hop in (*range(1, n_ctx), 0):
-            spread(kind, hop).start()
-
-    def sum_spread(kind):
-        for hop in range(n_ctx):
-            copy = spread(kind, hop)
-            if hop == 0:
-                copy.wait()
-            else:
-                copy.wait_recv()
+    def first_size(group):
+        return places[groups_of[group][4]][0]
+
+    def second_size(group):
+        return places[places[groups_of[group][4]][2]][0]
+
+    def start_first(group):
+        for hop in (*range(1, first_size(group)), 0):
+            first(group, hop).start()
+
+    def sum_first(group):
+        _, _, count, chunk, _ = groups_of[group]
+        first(group, 0).wait()
+        for hop in range(1, first_size(group)):
+            first(group, hop).wait_recv()
 
         def add(step, carry):
-            rows = pl.ds(pl.multiple_of(step * shard, 16), shard)
-            total = collected[kind, 0, rows, :].astype(F32)
-            for hop in range(1, n_ctx):
-                total = total + collected[kind, hop, rows, :].astype(F32)
-            pieces[kind, rows, :] = total.astype(BF16)
+            total = collected[0, chunk + step].astype(F32)
+            for hop in range(1, first_size(group)):
+                total = total + collected[hop, chunk + step].astype(F32)
+            pieces[chunk + step] = total.astype(BF16)
             return carry
 
-        lax.fori_loop(0, n_dp, add, 0)
-        for step in range(1, n_dp):
-            scatter(kind, step).start()
-
-    def sum_scatter(kind):
-        rows = pl.ds(pl.multiple_of(dp * shard, 16), shard)
-        total = pieces[kind, rows, :].astype(F32)
-        for step in range(1, n_dp):
-            scatter(kind, step).wait_recv()
-            total = total + scattered[kind, step].astype(F32)
-        final_ref[kind, ctx] = total.astype(BF16)
+        lax.fori_loop(0, count, add, 0)
+        for hop in range(1, second_size(group)):
+            second(group, hop).start()
+
+    def sum_second(group):
+        _, _, count, chunk, axis = groups_of[group]
+        own = places[places[axis][2]][1]
+        for hop in range(1, second_size(group)):
+            second(group, hop).wait_recv()
+        for number in range(chunk, chunk + count):
+            total = pieces[number, own].astype(F32)
+            for hop in range(1, second_size(group)):
+                total = total + gathered[hop, number].astype(F32)
+            final_ref[number, ctx] = total.astype(BF16)
         for hop in range(1, n_ctx):
-            regather(kind, hop, True).start()
+            third(group, hop, True).start()
+
+    if reduces:
+        start_first(outer_far)
+        start_first(inner_far)
 
     def project(step, carry):
         rows = rows_of(step)
@@ -793,10 +901,10 @@
             moved(pair, hop).start()
 
     if reduces:
-        start_spread(2)
-    for step in range(2):
-        rows = slice(step * width // 2, (step + 1) * width // 2)
-        proj_part_ref[3, rows, :] = dot_tn(branch_ref[:, rows], mixed_ref[...]).astype(BF16)
+        start_first(inner_near)
+    store_chunk(proj_part_ref, 0, dot_tn(branch_ref[...], mixed_ref[...]).astype(BF16))
+    if reduces:
+        start_first(0)
 
     def sent_back(pair, hop):
         target = lax.rem(ctx - hop + n_ctx, n_ctx)
@@ -852,8 +960,7 @@
             sent_back(pair, hop).start()
 
     if reduces:
-        start_spread(1)
-        sum_spread(2)
+        sum_first(0)
     for pair in range(pairs):
         for hop in range(n_ctx):
             copy = sent_back(pair, hop)
@@ -885,12 +992,16 @@
             return carry
 
         lax.fori_loop(0, n_ctx, restore, 0)
-
-    for number in range(3):
-        lanes = slice(number * columns, (number + 1) * columns)
-        proj_part_ref[number] = dot_tn(x_ref[...], restored[:, lanes]).astype(BF16)
-    if reduces:
-        start_spread(0)
+        grads = jnp.concatenate(
+            [
+                restored[:, number * columns + pair * PAIR : number * columns + (pair + 1) * PAIR]
+                for number in range(3)
+            ],
+            axis=1,
+        )
+        store_chunk(proj_part_ref, 1 + pair, dot_tn(x_ref[...], grads).astype(BF16))
+        if reduces:
+            start_first(1 + pair)
 
     def exchange(step):
         return remote(
@@ -940,31 +1051,41 @@
         input_grad_ref[rows, :] = (summed_ref[rows, :] + back).astype(BF16)
         return carry
 
+    if reduces:
+        sum_first(outer_far)
+        sum_first(inner_near)
     lax.fori_loop(0, n_ctx, take, 0)
 
     if reduces:
-        sum_scatter(2)
         for step in range(1, n_ctx):
             sums_out(0, step).wait_recv()
         sums[16:32, :] = jnp.sum(sums_ctx[...], axis=0)
         for step in range(1, n_dp):
             sums_out(1, step).start()
         sums_dp[dp] = sums[16:32, :]
-        sum_spread(1)
-        sum_spread(0)
+        for pair in range(pairs - 1):
+            sum_first(1 + pair)
+        sum_first(inner_far)
+        sum_first(pairs)
+        sum_second(outer_far)
+        sum_second(0)
+        sum_second(inner_near)
         for step in range(1, n_dp):
             sums_out(1, step).wait_recv()
         totals_ref[...] = jnp.sum(sums_dp[...], axis=0)
-        sum_scatter(1)
-        sum_scatter(0)
-        for kind in range(3):
+        for pair in range(pairs - 1):
+            sum_second(1 + pair)
+        sum_second(inner_far)
+        sum_second(pairs)
+        for group in range(4 + pairs):
             for hop in range(1, n_ctx):
-                regather(kind, hop, False).wait_recv()
+                third(group, hop, False).wait_recv()
             for hop in range(1, n_ctx):
-                spread(kind, hop).wait_send()
-                regather(kind, hop, True).wait_send()
-            for step in range(1, n_dp):
-                scatter(kind, step).wait_send()
+                third(group, hop, True).wait_send()
+            for hop in range(1, first_size(group)):
+                first(group, hop).wait_send()
+            for hop in range(1, second_size(group)):
+                second(group, hop).wait_send()
         for level, size in enumerate((n_ctx, n_dp)):
             for step in range(1, size):
                 sums_out(level, step).wait_send()
@@ -990,14 +1111,17 @@
     vmem = pl.BlockSpec(memory_space=pltpu.VMEM)
     hbm = pl.BlockSpec(memory_space=pl.ANY)
     dma = pltpu.SemaphoreType.DMA
-    kinds, steps = (3, n_dp) if reduces else (1, 2)
+    chunks, steps = (1 + pairs + 2 * n_ctx, n_dp) if reduces else (1, 1)
+    tile = shard // n_ctx if reduces else 16
+    total = 4 + pairs
+    hops = max(n_ctx, steps)
     return pl.pallas_call(
         functools.partial(backward_kernel, (n_dp, n_ctx, pairs, reduces)),
         out_shape=(
             jax.ShapeDtypeStruct((slab, width), BF16),
-            jax.ShapeDtypeStruct((kinds, n_ctx, shard, columns), BF16),
+            jax.ShapeDtypeStruct((chunks, n_ctx, tile, columns), BF16),
             jax.ShapeDtypeStruct((16, width), F32),
-            jax.ShapeDtypeStruct((4, width, columns), BF16),
+            jax.ShapeDtypeStruct(chunk_shape(1 + pairs, width, columns, reduces), BF16),
         ),
         in_specs=[vmem] * 8 + [hbm] * 2 + [vmem],
         out_specs=[vmem] * 4,
@@ -1008,9 +1132,9 @@
             pltpu.VMEM((pairs, groups, CLUSTER, 3 * PAIR), BF16),
             pltpu.VMEM((pairs, n_ctx, groups, share, 3 * PAIR), BF16),
             pltpu.VMEM((slab, 3 * columns), BF16),
-            pltpu.VMEM((kinds, n_ctx, width, columns), BF16),
-            pltpu.VMEM((kinds, width, columns), BF16),
-            pltpu.VMEM((kinds, steps, shard, columns), BF16),
+            pltpu.VMEM((hops, chunks, n_ctx, tile, columns), BF16),
+            pltpu.VMEM((chunks, n_ctx, tile, columns), BF16),
+            pltpu.VMEM((hops, chunks, tile, columns), BF16),
             pltpu.VMEM((slab, width), BF16),
             pltpu.VMEM((slab, width), BF16),
             pltpu.VMEM((32, width), F32),
@@ -1020,20 +1144,107 @@
             dma((pairs, n_ctx)),
             dma((pairs, n_ctx)),
             dma((pairs, n_ctx)),
-            dma((kinds, n_ctx)),
-            dma((kinds, n_ctx)),
-            dma((kinds, steps)),
-            dma((kinds, steps)),
-            dma((kinds, n_ctx)),
-            dma((kinds, n_ctx)),
-            dma((2, max(n_ctx, steps))),
-            dma((2, max(n_ctx, steps))),
+            dma((total, hops)),
+            dma((total, hops)),
+            dma((total, hops)),
+            dma((total, hops)),
+            dma((total, hops)),
+            dma((total, hops)),
+            dma((2, hops)),
+            dma((2, hops)),
             dma((n_ctx,)),
             dma((n_ctx,)),
         ],
         compiler_params=pltpu.CompilerParams(collective_id=2, has_side_effects=True),
         name="backward_attention",
     )(x, branch, summed, mixed, got, proj, cols, rows, inner_part, outer_part, sums)
+
+
+def results_kernel(
+    activations_in,
+    input_grad_in,
+    final_ref,
+    totals_ref,
+    activations_ref,
+    input_grad_ref,
+    query_ref,
+    key_ref,
+    value_ref,
+    output_ref,
+    inner_ref,
+    outer_ref,
+    query_bias_ref,
+    value_bias_ref,
+    output_bias_ref,
+    inner_bias_ref,
+    outer_bias_ref,
+    first_gain_ref,
+    first_shift_ref,
+    second_gain_ref,
+    second_shift_ref,
+):
+    chunks, blocks, tile, columns = final_ref.shape
+    width = totals_ref.shape[1]
+    pairs = columns // PAIR
+    strips = (chunks - 1 - pairs) // 2
+    activations_ref[...] = activations_in[...]
+    input_grad_ref[...] = input_grad_in[...]
+    for block in range(blocks):
+        rows = slice(block * tile, (block + 1) * tile)
+        output_ref[rows, :] = final_ref[0, block].astype(F32)
+        for pair in range(pairs):
+            lanes = slice(pair * PAIR, (pair + 1) * PAIR)
+            for number, ref in enumerate((query_ref, key_ref, value_ref)):
+                part = final_ref[1 + pair, block, :, number * PAIR : (number + 1) * PAIR]
+                ref[rows, lanes] = part.astype(F32)
+        for number, ref in enumerate((inner_ref, outer_ref)):
+            for strip in range(strips):
+                lanes = slice(strip * columns, (strip + 1) * columns)
+                chunk = 1 + pairs + number * strips + strip
+                ref[rows, lanes] = final_ref[chunk, block].astype(F32)
+    query_bias_ref[...] = totals_ref[8, :columns]
+    value_bias_ref[...] = totals_ref[8, columns:]
+    output_bias_ref[...] = totals_ref[7, :]
+    inner_bias_ref[:width] = totals_ref[0, :]
+    inner_bias_ref[width:] = totals_ref[1, :]
+    rest = (outer_bias_ref, first_gain_ref, first_shift_ref, second_gain_ref, second_shift_ref)
+    for number, ref in enumerate(rest):
+        ref[...] = totals_ref[2 + number, :]
+
+
+def write_results(activations, input_grad, final, totals):
+    chunks, blocks, tile, columns = final.shape
+    slab, width = activations.shape
+    shard = blocks * tile
+    hidden = (chunks - 1 - columns // PAIR) // 2 * columns
+    shapes = (
+        [(shard, columns)] * 4
+        + [(shard, hidden)] * 2
+        + [(columns,)] * 2
+        + [(width,), (hidden,)]
+        + [(width,)] * 5
+    )
+    vmem = pl.BlockSpec(memory_space=pltpu.VMEM)
+    results = pl.pallas_call(
+        results_kernel,
+        out_shape=[jax.ShapeDtypeStruct((slab, width), BF16)] * 2
+        + [jax.ShapeDtypeStruct(shape, F32) for shape in shapes],
+        in_specs=[vmem] * 4,
+        out_specs=[vmem] * 17,
+        name="write_results",
+    )(activations, input_grad, final, totals)
+    activations, input_grad, query, key, value, output, inner, outer = results[:8]
+    return (
+        activations[None],
+        input_grad[None],
+        query,
+        key,
+        value,
+        output.T,
+        inner,
+        outer.T,
+        *results[8:],
+    )
 
 
 def slot_tables(cluster_order, prefix_length, own, n_ctx):
@@ -1075,50 +1286,30 @@
     own = lax.axis_index("context")
     x = tokens[0]
     shard, columns = query_weight.shape
-    aligned = shard % 16 == 0
+    aligned = n_ctx == lax.axis_size("dp") and shard % (16 * n_ctx) == 0
     weights = (query_weight, key_weight, value_weight, output_weight.T, inner_weight, outer_weight.T)
     if not aligned:
         weights = tuple(lax.all_gather(w, "dp", axis=0, tiled=True) for w in weights)
     cols, rows = slot_tables(cluster_order, prefix_length, own, n_ctx)
-    biases = (query_bias[None], value_bias[None], output_bias[None])
+    biases = (query_bias, value_bias, output_bias)
+    vectors = (inner_bias, outer_bias, first_gain, first_shift, second_gain, second_shift)
     first_in, mixed, got, proj, inner_full, outer_full = forward_attention(
         x, weights, cols, rows, biases, aligned
     )
     if not aligned:
         inner_full, outer_full = weights[4:]
-    vectors = (inner_bias, outer_bias, first_gain, first_shift, second_gain, second_shift)
     activations, summed, branch, inner_part, outer_part, sums = feed_forward(
-        first_in, cotangent[0], inner_full, outer_full, tuple(v[None] for v in vectors)
+        first_in, cotangent[0], inner_full, outer_full, vectors, aligned
     )
     input_grad, final, totals, proj_part = backward_attention(
         x, branch, summed, mixed, got, proj, cols, rows, inner_part, outer_part, sums, aligned
     )
     if not aligned:
-        parts = jnp.stack((proj_part, inner_part, outer_part))
-        piece = lax.psum_scatter(parts, "dp", scatter_dimension=2, tiled=True)
-        final = lax.psum(piece, "context")
+        parts = jnp.concatenate((proj_part, inner_part, outer_part), axis=0)
+        piece = lax.psum_scatter(parts, "dp", scatter_dimension=1, tiled=True)
+        final = lax.psum(piece, "context")[:, None]
         totals = lax.psum(totals, ("dp", "context"))
-    final = final.astype(F32)
-    wide = final.transpose(0, 2, 1, 3).reshape(3, shard, n_ctx * columns)
-    return (
-        activations[None],
-        input_grad[None],
-        final[0, 0],
-        final[0, 1],
-        final[0, 2],
-        final[0, 3].T,
-        wide[1],
-        wide[2].T,
-        totals[8, :columns],
-        totals[8, columns:],
-        totals[7],
-        totals[0:2].reshape(-1),
-        totals[2],
-        totals[3],
-        totals[4],
-        totals[5],
-        totals[6],
-    )
+    return write_results(activations, input_grad, final, totals)
 
 
 def solution(mesh):

time: 358 us -> 263 us (0.73)
  Pallas kernels: 325 us -> 256 us
  local copies, waits for them, and re-layouts: 25.8 us -> 2.17 us
    pallas_call x1, Pallas kernels: 173 us -> 124 us  [backward_attention(): pl.pallas_call(functools.partial(backward_kernel, (n_dp, n_ctx, pairs, re...]
    pallas_call x1, Pallas kernels: 117 us -> 91.7 us  [forward_attention(): pl.pallas_call(functools.partial(forward_kernel, (n_dp, n_ctx, pairs, gat...]
    broadcast_in_dim x9 -> x0, local copies, waits for them, and re-layouts: 11.4 us -> none  [the longest x6 7.63 us: shards(): v[None]]
    pallas_call x0 -> x1, Pallas kernels: none -> 5.38 us  [write_results(): pl.pallas_call(results_kernel, out_shape=[jax.ShapeDtypeStruct((slab, wid...]
    slice x6 -> x0, local copies, waits for them, and re-layouts: 5.37 us -> none  [the longest x1 1.62 us: shards(): totals[6]]
    unnamed x9 -> x1, local copies, waits for them, and re-layouts: 5.29 us -> 0.01 us
where the time goes in v3:
time: 263 us; the launch traced here: 262 us
  Pallas kernels  256 us (97%)
    pallas_call x1, Pallas kernels, backward_attention(): pl.pallas_call(functools.partial(backward_kernel, (n_dp, n_ctx, pairs, re...  124 us
    pallas_call x1, Pallas kernels, forward_attention(): pl.pallas_call(functools.partial(forward_kernel, (n_dp, n_ctx, pairs, gat...  91.7 us
    pallas_call x1, Pallas kernels, feed_forward(): pl.pallas_call(functools.partial(feed_kernel, blocks), out_shape=(jax.Sha...  35.3 us
    pallas_call x1, Pallas kernels, write_results(): pl.pallas_call(results_kernel, out_shape=[jax.ShapeDtypeStruct((slab, wid...  5.38 us

profile of v3, /device:TPU:0, one launch (start us, length us, event | category | flops | bytes accessed | tf_op | source)
XLA Modules:
  0.0 261.6 jit_solution(15400869533460824654)
XLA Ops:
  1.3 0.7 constant_dynamic-slice_fusion
  2.1 1.1 reduce
  3.2 0.2 reshape.44
  3.4 0.1 constant_dynamic-slice_fusion.1
  3.6 0.1 sub.16
  3.7 0.7 pad_add_fusion
  4.3 1.0 copy.37.cols_ref
  5.3 91.7 %forward_attention.1 = (f32[1024,768]{1,0:T(8,128)}, bf16[1024,384]{1,0:T(8,128)(2,1)}, bf16[3,8,128,384]{3,2,1,0:T(8,128)(2,1)}, bf16[768,1536]{1,0:T(8,128)(2,...) custom-call(bf16[1024,768]{1,0:T(8,128)(2,1)} %bitcast.21, bf16[192,384]{1,0:T(8,128)(2,1)} %query_ref.1, ...), custom_call_target="tpu_custom_call" | custom-call | tf_op jit(solution)/shard_map/forward_attention/pallas_call | solution.py:494
  97.0 35.3 %feed_forward.1 = (bf16[1024,768]{1,0:T(8,128)(2,1)}, f32[1024,768]{1,0:T(8,128)}, bf16[1024,768]{1,0:T(8,128)(2,1)}, bf16[4,4,4,48,384]{4,3,2,1,0:T(8,128)(2,1)...) custom-call(f32[1024,768]{1,0:T(8,128)} %get-tuple-element.49.first_in_ref, bf16[1024,768]{1,0:T(8,128)(2,1)} %bitcast.23, ...), custom_call_target="tpu_custom_call" | custom-call | tf_op jit(solution)/shard_map/feed_forward/pallas_call | solution.py:689
  132.3 123.7 %backward_attention.1 = (bf16[1024,768]{1,0:T(8,128)(2,1)}, bf16[12,4,48,384]{3,2,1,0:T(8,128)(2,1)}, f32[16,768]{1,0:T(8,128)}, bf16[4,4,4,48,384]{4,3,2,1,0:T(8,128)(2,1)}) custom-call(bf16[1024,768]{1,0:T(8,128)(2,1)} %bitcast.22, bf16[1024,768]{1,0:T(8,128)(2,1)} %get-tuple-element.53.branch_ref, f32[1024,768]{1,0:T(8,128)} %get-tuple-element.54.summed_ref, ...), custom_call_target="tpu_custom_call" | custom-call | tf_op jit(solution)/shard_map/backward_attention/pallas_call | solution.py:1118
  256.0 5.4 %write_results.1 = (bf16[1024,768]{1,0:T(8,128)(2,1)}, bf16[1024,768]{1,0:T(8,128)(2,1)}, f32[192,384]{1,0:T(8,128)}, f32[192,384]{1,0:T(8,128)}, f32[192,384]{1...) custom-call(bf16[1024,768]{1,0:T(8,128)(2,1)} %get-tuple-element.52., ...), custom_call_target="tpu_custom_call" | custom-call | tf_op jit(solution)/shard_map/write_results/pallas_call | solution.py:1228
  (4 shorter events, 0.0 us)

commit v4 on v3

--- a/solution.py
+++ b/solution.py
@@ -54,6 +54,19 @@
         device_id={axis: index},
         device_id_type=MESH,
     )
+
+
+def partner(own, hop, size):
+    place, bit = own, 1
+    while bit < size:
+        if hop & bit:
+            place = place + bit * (1 - 2 * lax.rem(lax.div(own, bit), 2))
+        bit *= 2
+    return place
+
+
+def peer(axis, own, hop, size):
+    return partner(own, hop, size) if axis == "context" else lax.rem(own + hop, size)
 
 
 def meet(axes):
@@ -246,7 +259,7 @@
                     inner_forward.at[step, hop],
                     inner_recv.at[ctx, source],
                     "context",
-                    lax.rem(ctx + hop, n_ctx),
+                    partner(ctx, hop, n_ctx),
                 )
                 copy.start()
                 feed_copies.append(copy)
@@ -268,12 +281,12 @@
                     forward_send.at[step, hop],
                     gather_recv.at[ctx, source],
                     "context",
-                    lax.rem(ctx + hop, n_ctx),
+                    partner(ctx, hop, n_ctx),
                 )
                 copy.start()
                 gather_copies.append(copy)
         for hop in range(1, n_ctx):
-            other = lax.rem(ctx - hop + n_ctx, n_ctx)
+            other = partner(ctx, hop, n_ctx)
             for step in range(1, n_dp):
                 source = lax.rem(dp - step + n_dp, n_dp)
                 remote(
@@ -335,7 +348,7 @@
             ).reshape(groups, share, PAIR)
 
     def moved(pair, hop):
-        target = lax.rem(ctx + hop, n_ctx)
+        target = partner(ctx, hop, n_ctx)
         source = sending.at[pair, target]
         landing = got_ref.at[pair, :, own_share, :]
         if hop == 0:
@@ -346,11 +359,11 @@
 
     for pair in range(pairs):
         for hop in (*range(1, n_ctx), 0):
-            pick(pair, lax.rem(ctx + hop, n_ctx))
+            pick(pair, partner(ctx, hop, n_ctx))
             moved(pair, hop).start()
 
     def sent_back(pair, hop):
-        target = lax.rem(ctx - hop + n_ctx, n_ctx)
+        target = partner(ctx, hop, n_ctx)
         rows = pl.ds(pl.multiple_of(target * share, share), share)
         source = answer.at[pair, :, rows, :]
         landing = returned.at[pair, ctx]
@@ -461,7 +474,7 @@
                 source,
             ).wait_recv()
             for hop in range(1, n_ctx):
-                other = lax.rem(ctx - hop + n_ctx, n_ctx)
+                other = partner(ctx, hop, n_ctx)
                 remote(
                     strip(source, other),
                     strip(source, other),
@@ -786,7 +799,7 @@
     def first(group, hop):
         source, start, count, chunk, axis = groups_of[group]
         size, own, _ = places[axis]
-        target = lax.rem(own + hop, size)
+        target = peer(axis, own, hop, size)
         if axis == "context":
             sent = source.at[start : start + count, target]
         else:
@@ -802,7 +815,7 @@
         _, _, count, chunk, axis = groups_of[group]
         other = places[axis][2]
         size, own, _ = places[other]
-        target = lax.rem(own + hop, size)
+        target = peer(other, own, hop, size)
         return remote(
             pieces.at[chunk : chunk + count, target],
             gathered.at[hop, chunk : chunk + count],
@@ -814,7 +827,7 @@
 
     def third(group, hop, mine):
         _, _, count, chunk, _ = groups_of[group]
-        owner = ctx if mine else lax.rem(ctx - hop + n_ctx, n_ctx)
+        owner = ctx if mine else partner(ctx, hop, n_ctx)
         block = final_ref.at[chunk : chunk + count, owner]
         return remote(
             block,
@@ -822,7 +835,7 @@
             third_send.at[group, hop],
             third_recv.at[group, hop],
             "context",
-            lax.rem(ctx + hop, n_ctx),
+            partner(ctx, hop, n_ctx),
         )
 
     def first_size(group):
@@ -879,7 +892,7 @@
     own_share = pl.ds(pl.multiple_of(ctx * share, share), share)
 
     def moved(pair, hop):
-        target = lax.rem(ctx + hop, n_ctx)
+        target = partner(ctx, hop, n_ctx)
         source = sending.at[pair, target]
         landing = landed.at[pair, :, own_share, :]
         if hop == 0:
@@ -890,7 +903,7 @@
 
     for pair in range(pairs):
         for hop in (*range(1, n_ctx), 0):
-            target = lax.rem(ctx + hop, n_ctx)
+            target = partner(ctx, hop, n_ctx)
             rows = rows_of(target)
             positions = lax.broadcasted_iota(jnp.int32, (chunk, slab), 1)
             values = upstream[:, pair * PAIR : (pair + 1) * PAIR]
@@ -907,7 +920,7 @@
         start_first(0)
 
     def sent_back(pair, hop):
-        target = lax.rem(ctx - hop + n_ctx, n_ctx)
+        target = partner(ctx, hop, n_ctx)
         rows = pl.ds(pl.multiple_of(target * share, share), share)
         source = answer.at[pair, :, rows, :]
         landing = returned.at[pair, ctx]

time: 263 us -> 264 us (level)
  no operation moved by 1% of the time
where the time goes in v4:
time: 264 us; the launch traced here: 262 us
  Pallas kernels  257 us (97%)
    pallas_call x1, Pallas kernels, backward_attention(): pl.pallas_call(functools.partial(backward_kernel, (n_dp, n_ctx, pairs, re...  124 us
    pallas_call x1, Pallas kernels, forward_attention(): pl.pallas_call(functools.partial(forward_kernel, (n_dp, n_ctx, pairs, gat...  91.9 us
    pallas_call x1, Pallas kernels, feed_forward(): pl.pallas_call(functools.partial(feed_kernel, blocks), out_shape=(jax.Sha...  35.3 us
    pallas_call x1, Pallas kernels, write_results(): pl.pallas_call(results_kernel, out_shape=[jax.ShapeDtypeStruct((slab, wid...  5.38 us

profile of v4, /device:TPU:0, one launch (start us, length us, event | category | flops | bytes accessed | tf_op | source)
XLA Modules:
  0.0 262.2 jit_solution(18394127481075071492)
XLA Ops:
  1.3 0.7 constant_dynamic-slice_fusion
  2.1 1.1 reduce
  3.2 0.2 reshape.44
  3.4 0.1 constant_dynamic-slice_fusion.1
  3.6 0.1 sub.16
  3.7 0.7 pad_add_fusion
  4.3 1.0 copy.37.cols_ref
  5.3 91.9 %forward_attention.1 = (f32[1024,768]{1,0:T(8,128)}, bf16[1024,384]{1,0:T(8,128)(2,1)}, bf16[3,8,128,384]{3,2,1,0:T(8,128)(2,1)}, bf16[768,1536]{1,0:T(8,128)(2,...) custom-call(bf16[1024,768]{1,0:T(8,128)(2,1)} %bitcast.21, bf16[192,384]{1,0:T(8,128)(2,1)} %query_ref.1, ...), custom_call_target="tpu_custom_call" | custom-call | tf_op jit(solution)/shard_map/forward_attention/pallas_call | solution.py:507
  97.2 35.3 %feed_forward.1 = (bf16[1024,768]{1,0:T(8,128)(2,1)}, f32[1024,768]{1,0:T(8,128)}, bf16[1024,768]{1,0:T(8,128)(2,1)}, bf16[4,4,4,48,384]{4,3,2,1,0:T(8,128)(2,1)...) custom-call(f32[1024,768]{1,0:T(8,128)} %get-tuple-element.49.first_in_ref, bf16[1024,768]{1,0:T(8,128)(2,1)} %bitcast.23, ...), custom_call_target="tpu_custom_call" | custom-call | tf_op jit(solution)/shard_map/feed_forward/pallas_call | solution.py:702
  132.5 124.1 %backward_attention.1 = (bf16[1024,768]{1,0:T(8,128)(2,1)}, bf16[12,4,48,384]{3,2,1,0:T(8,128)(2,1)}, f32[16,768]{1,0:T(8,128)}, bf16[4,4,4,48,384]{4,3,2,1,0:T(8,128)(2,1)}) custom-call(bf16[1024,768]{1,0:T(8,128)(2,1)} %bitcast.22, bf16[1024,768]{1,0:T(8,128)(2,1)} %get-tuple-element.53.branch_ref, f32[1024,768]{1,0:T(8,128)} %get-tuple-element.54.summed_ref, ...), custom_call_target="tpu_custom_call" | custom-call | tf_op jit(solution)/shard_map/backward_attention/pallas_call | solution.py:1131
  256.6 5.4 %write_results.1 = (bf16[1024,768]{1,0:T(8,128)(2,1)}, bf16[1024,768]{1,0:T(8,128)(2,1)}, f32[192,384]{1,0:T(8,128)}, f32[192,384]{1,0:T(8,128)}, f32[192,384]{1...) custom-call(bf16[1024,768]{1,0:T(8,128)(2,1)} %get-tuple-element.52., ...), custom_call_target="tpu_custom_call" | custom-call | tf_op jit(solution)/shard_map/write_results/pallas_call | solution.py:1241
  (4 shorter events, 0.0 us)
